TPU v7x, 32 devices: a whole 2x2x4 slice. The times are simulated.
32 devices in a mesh: dp: 2 (over x), ctx: 4 (over y, core), tensor: 4 (over z).
Axes of the slice: x: 2, y: 2, z: 4, core: 2. Of those that a mesh axis runs over, the one named last changes fastest.
Arguments:
- tokens: bfloat16 [2, 4096, 768], P('dp', 'ctx'), may hold values from -6 to 6
- segment_ids: int32 [2, 4096], P('dp'), may hold values from 0 to 4, never falling along the last dimension, each value on 1 to 2000 neighbouring positions
- routes: int32 [2, 4096, 2], P('dp', 'ctx'), may hold values from 0 to 15, all different within a row
- pair_order: int32 [2, 4, 2048], P('dp', 'ctx'), may hold values from 0 to 2047, each once within a row
- gain_attn: bfloat16 [768], P(('dp', 'ctx')), may hold values from 0.099609375 to 1.8984375
- qkv_weight: bfloat16 [3, 768, 768], P(None, ('dp', 'ctx'), 'tensor'), may hold values from -0.21875 to 0.21875
- out_weight: bfloat16 [768, 768], P(('dp', 'ctx'), 'tensor'), may hold values from -2 to 2
- gain_ffn: bfloat16 [768], P(('dp', 'ctx')), may hold values from 0.099609375 to 1.8984375
- router_weight: bfloat16 [768, 16], P(('dp', 'ctx')), may hold values from -0.15625 to 0.15625
- shared_in: bfloat16 [2, 768, 2048], P(None, ('dp', 'ctx'), 'tensor'), may hold values from -0.21875 to 0.21875
- shared_out: bfloat16 [768, 2048], P(('dp', 'ctx'), 'tensor'), may hold values from -0.125 to 0.125
- expert_in: bfloat16 [16, 2, 768, 2048], P('dp', None, 'ctx', 'tensor'), may hold values from -0.21875 to 0.21875
- expert_out: bfloat16 [16, 768, 2048], P('dp', 'ctx', 'tensor'), may hold values from -0.125 to 0.125
- out_grad: bfloat16 [2, 4096, 768], P('dp', 'ctx'), may hold values from -6 to 6
Outputs:
- layer_out: bfloat16 [2, 4096, 768], P('dp', 'ctx')
- grad_tokens: float32 [2, 4096, 768], P('dp', 'ctx')
- grad_gain_attn: float32 [768], P(('dp', 'ctx'))
- grad_qkv: float32 [3, 768, 768], P(None, ('dp', 'ctx'), 'tensor')
- grad_out_weight: float32 [768, 768], P(('dp', 'ctx'), 'tensor')
- grad_gain_ffn: float32 [768], P(('dp', 'ctx'))
- grad_router: float32 [768, 16], P(('dp', 'ctx'))
- grad_shared_in: float32 [2, 768, 2048], P(None, ('dp', 'ctx'), 'tensor')
- grad_shared_out: float32 [768, 2048], P(('dp', 'ctx'), 'tensor')
- grad_expert_in: float32 [16, 2, 768, 2048], P('dp', None, 'ctx', 'tensor')
- grad_expert_out: float32 [16, 768, 2048], P('dp', 'ctx', 'tensor')
Inputs may be any that keep to these rules, and one draw needn't show every extreme that they name: `segment_ids`: along a sequence the document numbers never fall; a document spans at most 2000 consecutive tokens, and in every sequence one spans exactly that many. The two routes of a token name different experts. `pair_order`: for every sequence and routing group, a permutation of the numbers of its 2048 pairs.
All inputs are finite; a program needn't handle non-finite values.
Results may differ from a plain program's by a relative error of at most 0.015.
Values may be sent and summed in bfloat16 or wider, within the bound.
No kernel may reach another device: no remote copies, remote signals or barrier semaphores. Data moves between devices by JAX's collectives and lax.ppermute only.
A program may use at most 256 MiB of HBM per device.

v0:
```python
import functools
import math

import jax
import jax.numpy as jnp
from jax import lax
from jax.experimental import pallas as pl
from jax.experimental.layout import Layout, with_layout_constraint
from jax.experimental.pallas import tpu as pltpu
from jax.sharding import PartitionSpec as P


HD = 64
HALF = HD // 2
EPSILON = 1e-06
LONGEST = 2000
DOCS = 5
BQ = 512
BK = 256
BF = jnp.bfloat16
F32 = jnp.float32
NEG = -1e30
DC = ("dp", "ctx")


def mm(a, b, ca, cb):
    return lax.dot_general(a, b, (((ca,), (cb,)), ((), ())), preferred_element_type=F32)


def attn_mask(key_start, query_start, doc_row):
    kpos = key_start + lax.broadcasted_iota(jnp.int32, (BK, BQ), 0)
    qpos = query_start + lax.broadcasted_iota(jnp.int32, (BK, BQ), 1)
    return (kpos <= qpos) & (kpos >= doc_row)


def attn_fwd_kernel(lo_ref, q_ref, k_ref, v_ref, doc_ref, o_ref, lse_ref, *, shift):
    cols, rows = q_ref.shape
    heads = [slice(at, at + HD) for at in range(0, cols, HD)]
    for qb in range(rows // BQ):
        here = slice(qb * BQ, (qb + 1) * BQ)
        qs = [q_ref[h, here] * 0.125 for h in heads]
        doc = doc_ref[:, here]
        q0 = shift + qb * BQ

        def step(b, carry, qs=qs, doc=doc, q0=q0):
            off = pl.multiple_of(b * BK, BK)
            mask = attn_mask(off, q0, doc)
            scores = [
                jnp.where(mask, mm(k_ref[h, pl.ds(off, BK)], q, 0, 0), NEG)
                for h, q in zip(heads, qs)
            ]
            out = []
            for h, s, (peak, total, acc) in zip(heads, scores, carry):
                new = jnp.maximum(peak, jnp.max(s, axis=0, keepdims=True))
                p = jnp.exp(s - new)
                fix = jnp.exp(peak - new)
                total = total * fix + jnp.sum(p, axis=0, keepdims=True)
                acc = acc * fix + mm(v_ref[h, pl.ds(off, BK)], p.astype(BF), 1, 0)
                out.append((new, total, acc))
            return tuple(out)

        init = tuple(
            (
                jnp.full((1, BQ), NEG, F32),
                jnp.zeros((1, BQ), F32),
                jnp.zeros((HD, BQ), F32),
            )
            for _ in heads
        )
        last = (q0 + BQ - 1) // BK
        carry = step(last, init)
        carry = lax.fori_loop(lo_ref[qb], last, step, carry)
        for n, (h, (peak, total, acc)) in enumerate(zip(heads, carry)):
            o_ref[h, here] = (acc / total).astype(BF)
            lse_ref[n : n + 1, here] = peak + jnp.log(total)


def attn_bwd_kernel(
    lo_ref, q_ref, k_ref, v_ref, o_ref, do_ref, lse_ref, doc_ref, dq_ref, dk_ref, dv_ref, *, shift
):
    cols, rows = q_ref.shape
    heads = [slice(at, at + HD) for at in range(0, cols, HD)]
    dk_ref[...] = jnp.zeros_like(dk_ref)
    dv_ref[...] = jnp.zeros_like(dv_ref)
    for qb in range(rows // BQ):
        here = slice(qb * BQ, (qb + 1) * BQ)
        qs = [q_ref[h, here] * 0.125 for h in heads]
        dos = [do_ref[h, here] for h in heads]
        doc = doc_ref[:, here]
        lses = [lse_ref[n : n + 1, here] for n in range(len(heads))]
        deltas = [
            jnp.sum(do.astype(F32) * o_ref[h, here].astype(F32), axis=0, keepdims=True)
            for h, do in zip(heads, dos)
        ]
        q0 = shift + qb * BQ

        def step(b, dqs, qs=qs, dos=dos, doc=doc, lses=lses, deltas=deltas, q0=q0):
            off = pl.multiple_of(b * BK, BK)
            keys = pl.ds(off, BK)
            mask = attn_mask(off, q0, doc)
            scores = [
                jnp.where(mask, mm(k_ref[h, keys], q, 0, 0), NEG) for h, q in zip(heads, qs)
            ]
            dps = [mm(v_ref[h, keys], do, 0, 0) for h, do in zip(heads, dos)]
            out = []
            for n, h in enumerate(heads):
                p = jnp.exp(scores[n] - lses[n])
                ds = (p * (dps[n] - deltas[n])).astype(BF)
                dk_ref[h, keys] += mm(qs[n], ds, 1, 1)
                dv_ref[h, keys] += mm(dos[n], p.astype(BF), 1, 1)
                out.append(dqs[n] + mm(k_ref[h, keys], ds, 1, 0))
            return tuple(out)

        last = (q0 + BQ - 1) // BK
        zero = tuple(jnp.zeros((HD, BQ), F32) for _ in heads)
        dqs = lax.fori_loop(lo_ref[qb], last + 1, step, zero)
        for h, dq in zip(heads, dqs):
            dq_ref[h, here] = dq * 0.125


def whole(shape):
    return pl.BlockSpec(shape, lambda n, lo: (0, 0))


def attn_forward(lo, q_t, k_t, v_t, doc, shift):
    heads, rows = q_t.shape[0] // HD, q_t.shape[1]
    ins = (q_t, k_t, v_t, doc)
    outs = (
        jax.ShapeDtypeStruct(q_t.shape, BF),
        jax.ShapeDtypeStruct((heads, rows), F32),
    )
    return pl.pallas_call(
        functools.partial(attn_fwd_kernel, shift=shift),
        out_shape=outs,
        grid_spec=pltpu.PrefetchScalarGridSpec(
            num_scalar_prefetch=1,
            grid=(1,),
            in_specs=[whole(v.shape) for v in ins],
            out_specs=[whole(v.shape) for v in outs],
        ),
        name="attn_fwd",
    )(lo, *ins)


def attn_backward(lo, q_t, k_t, v_t, o_t, do_t, lse, doc, shift):
    ins = (q_t, k_t, v_t, o_t, do_t, lse, doc)
    outs = (
        jax.ShapeDtypeStruct(q_t.shape, F32),
        jax.ShapeDtypeStruct(k_t.shape, F32),
        jax.ShapeDtypeStruct(k_t.shape, F32),
    )
    return pl.pallas_call(
        functools.partial(attn_bwd_kernel, shift=shift),
        out_shape=outs,
        grid_spec=pltpu.PrefetchScalarGridSpec(
            num_scalar_prefetch=1,
            grid=(1,),
            in_specs=[whole(v.shape) for v in ins],
            out_specs=[whole(v.shape) for v in outs],
        ),
        name="attn_bwd",
    )(lo, *ins)


def ffn_kernel(*refs, gated):
    if gated:
        first_ref, x_ref, g_ref, other_ref, router_ref, win_ref, wout_ref = refs[:7]
        y_ref, dx_ref, gin_ref, gout_ref, grouter_ref, acc_in, acc_out, acc_router = refs[7:]
    else:
        x_ref, g_ref, win_ref, wout_ref = refs[:4]
        y_ref, dx_ref, gin_ref, gout_ref, acc_in, acc_out = refs[4:]
    src, _, rows, width = x_ref.shape
    expert, step = pl.program_id(0), pl.program_id(1)

    @pl.when(step == 0)
    def _():
        acc_in[...] = jnp.zeros_like(acc_in)
        acc_out[...] = jnp.zeros_like(acc_out)

    if gated:

        @pl.when((step == 0) & (expert == 0))
        def _():
            acc_router[...] = jnp.zeros_like(acc_router)

    x = x_ref[...].reshape(src * rows, width)
    g = g_ref[...].reshape(src * rows, width)
    w_gate = win_ref[0, 0]
    w_up = win_ref[0, 1]
    w_out = wout_ref[0]
    gate_pre = mm(x, w_gate, 1, 0)
    up_pre = mm(x, w_up, 1, 0)
    sig = 1.0 / (1.0 + jnp.exp(-gate_pre))
    silu = gate_pre * sig
    hidden = (silu * up_pre).astype(BF)
    y = mm(hidden, w_out, 1, 1)
    if gated:
        router = router_ref[...]
        logits = mm(x, router, 1, 0)
        ids = lax.broadcasted_iota(jnp.int32, logits.shape, 1)
        here = ids == first_ref[0] + expert
        there = ids == other_ref[...].reshape(src * rows, 1)
        apart = jnp.sum(
            jnp.where(here, logits, 0.0) - jnp.where(there, logits, 0.0), axis=1, keepdims=True
        )
        gate = 1.0 / (1.0 + jnp.exp(-apart))
        gate_other = 1.0 / (1.0 + jnp.exp(apart))
        gf = g.astype(F32)
        dpair = gate * gate_other * jnp.sum(gf * y, axis=1, keepdims=True)
        dlogits = (jnp.where(here, dpair, 0.0) - jnp.where(there, dpair, 0.0)).astype(BF)
        acc_router[...] += mm(x, dlogits, 0, 0)
        dy = (gate * gf).astype(BF)
        y = gate * y
    else:
        dy = g
    y_ref[...] = y.astype(BF).reshape(src, 1, rows, width)
    dh = mm(dy, w_out, 1, 0)
    dgp = (dh * up_pre * (sig * (1.0 + gate_pre * (1.0 - sig)))).astype(BF)
    dup = (dh * silu).astype(BF)
    dx = mm(dgp, w_gate, 1, 1) + mm(dup, w_up, 1, 1)
    if gated:
        dx = dx + mm(dlogits, router, 1, 1)
    dx_ref[...] = dx.astype(BF).reshape(src, 1, rows, width)
    acc_in[0] += mm(x, dgp, 0, 0)
    acc_in[1] += mm(x, dup, 0, 0)
    acc_out[...] += mm(dy, hidden, 0, 0)

    @pl.when(step == pl.num_programs(1) - 1)
    def _():
        gin_ref[0] = acc_in[...].astype(BF)
        gout_ref[0] = acc_out[...].astype(BF)
        if gated:
            grouter_ref[...] = acc_router[...]


def ffn(x, g, w_in, w_out, block, routing=None):
    sources, experts, rows, width = x.shape
    units = w_out.shape[2]
    gated = routing is not None
    block = math.gcd(sources, block)
    big = pl.BlockSpec((block, 1, rows, width), lambda e, s, *_: (s, e, 0, 0))
    w_in_spec = pl.BlockSpec((1, 2, width, units), lambda e, s, *_: (e, 0, 0, 0))
    w_out_spec = pl.BlockSpec((1, width, units), lambda e, s, *_: (e, 0, 0))
    wide = jax.ShapeDtypeStruct(x.shape, BF)
    ins = [x, g]
    in_specs = [big, big]
    outs = [
        wide,
        wide,
        jax.ShapeDtypeStruct((experts, 2, width, units), BF),
        jax.ShapeDtypeStruct((experts, width, units), BF),
    ]
    out_specs = [big, big, w_in_spec, w_out_spec]
    scratch = [pltpu.VMEM((2, width, units), F32), pltpu.VMEM((width, units), F32)]
    if gated:
        first, other, router = routing
        router_spec = pl.BlockSpec(router.shape, lambda e, s, *_: (0, 0))
        ins = [first] + ins + [other, router]
        in_specs += [pl.BlockSpec((block, 1, rows, 1), lambda e, s, *_: (s, e, 0, 0)), router_spec]
        outs.append(jax.ShapeDtypeStruct(router.shape, F32))
        out_specs.append(router_spec)
        scratch.append(pltpu.VMEM(router.shape, F32))
    return pl.pallas_call(
        functools.partial(ffn_kernel, gated=gated),
        out_shape=outs,
        grid_spec=pltpu.PrefetchScalarGridSpec(
            num_scalar_prefetch=1 if gated else 0,
            grid=(experts, sources // block),
            in_specs=in_specs + [w_in_spec, w_out_spec],
            out_specs=out_specs,
            scratch_shapes=scratch,
        ),
        compiler_params=pltpu.CompilerParams(
            dimension_semantics=("arbitrary", "arbitrary"), vmem_limit_bytes=56 * 1024 * 1024
        ),
        name="ffn_experts" if gated else "ffn_shared",
    )(*ins, w_in, w_out)


def tie(*values):
    return lax.optimization_barrier(values)


def pair_slots(pair_route, order, experts, capacity):
    count = order.shape[0]
    flat = pair_route.reshape(count)
    number = jnp.arange(count, dtype=jnp.int32)
    ids = jnp.arange(experts, dtype=jnp.int32)
    owner = (flat[:, None] == ids[None, :]).astype(BF)
    ranked = jnp.dot(
        (order[:, None] == number[None, :]).astype(BF), owner, preferred_element_type=F32
    ).astype(BF)
    earlier = jnp.dot(
        (number[None, :] < number[:, None]).astype(BF), ranked, preferred_element_type=F32
    )
    ranked_slot = (jnp.minimum(earlier, float(capacity)) * ranked).astype(BF)
    slot = jnp.sum(
        jnp.dot(
            (order[None, :] == number[:, None]).astype(BF),
            ranked_slot,
            preferred_element_type=F32,
        ),
        axis=1,
    ).astype(jnp.int32)
    place = jnp.where(slot < capacity, flat * capacity + slot, experts * capacity)
    return place.reshape(pair_route.shape)


def own_sum(parts, axis):
    devices = lax.axis_size(DC)
    shape = parts.shape
    cut = shape[:axis] + (devices, shape[axis] // devices) + shape[axis + 1 :]
    swapped = lax.all_to_all(
        parts.astype(BF).reshape(cut), DC, split_axis=axis, concat_axis=axis, tiled=True
    )
    return jnp.sum(swapped.astype(F32), axis=axis)


def half_turn(values_t, cos_t, sin_t):
    cols, rows = values_t.shape
    split = values_t.reshape(cols // HD, 2, HALF, rows)
    a, b = split[:, 0], split[:, 1]
    return jnp.stack([a * cos_t - b * sin_t, b * cos_t + a * sin_t], axis=1).reshape(cols, rows)


def shards(
    tokens,
    segment_ids,
    routes,
    pair_order,
    gain_attn,
    qkv_weight,
    out_weight,
    gain_ffn,
    router_weight,
    shared_in,
    shared_out,
    expert_in,
    expert_out,
    out_grad,
):
    rows, width = tokens.shape[1], tokens.shape[2]
    ctx_count = lax.axis_size("ctx")
    ctx_at = lax.axis_index("ctx")
    inputs = tokens[0].astype(F32)
    grad_low = out_grad[0]
    grad_layer = grad_low.astype(F32)
    seg_all = segment_ids[0]
    my_routes = routes[0]

    heads_cols = qkv_weight.shape[2]
    qkv_cols = 3 * heads_cols
    experts = router_weight.shape[1]
    thin = jnp.concatenate(
        [
            qkv_weight.transpose(1, 0, 2).reshape(-1, qkv_cols),
            out_weight,
            router_weight,
            gain_attn[:, None],
            gain_ffn[:, None],
        ],
        axis=1,
    )
    thin_full = lax.all_gather(thin, DC, axis=0, tiled=True)
    qkv_full = thin_full[:, :qkv_cols]
    out_full = thin_full[:, qkv_cols : qkv_cols + heads_cols]
    out_tensor = lax.all_gather(out_full, "tensor", axis=0)
    router_full = thin_full[:, qkv_cols + heads_cols : qkv_cols + heads_cols + experts]
    attn_gain = thin_full[:, -2].astype(F32)
    ffn_gain = thin_full[:, -1].astype(F32)

    local_experts = expert_in.shape[0]
    spread = local_experts % ctx_count == 0
    expert_axes = DC if spread else ("dp",)
    owners = lax.axis_size(expert_axes)
    own = experts // owners
    capacity = 10 * rows // (4 * experts)

    def swap(values):
        return lax.all_to_all(values, expert_axes, split_axis=0, concat_axis=0, tiled=True)

    place = pair_slots(my_routes, pair_order[0, 0], experts, capacity)
    block_ids = [
        (
            jnp.arange(owners, dtype=jnp.int32)[:, None] * (own * capacity)
            + (n * capacity + jnp.arange(capacity, dtype=jnp.int32))[None, :]
        ).reshape(-1)
        for n in range(own)
    ]
    owner_at = lax.axis_index(expert_axes)
    first = owner_at * own
    my_slots = first * capacity + jnp.arange(own * capacity, dtype=jnp.int32)
    pairs = lax.all_gather(
        jnp.stack([place[:, 0], place[:, 1], my_routes[:, 1], my_routes[:, 0]]),
        expert_axes,
        axis=0,
    )
    slot_other = (
        jnp.sum(
            jnp.where(
                pairs[:, :2, None, :] == my_slots[None, None, :, None],
                pairs[:, 2:, None, :] + 1,
                0,
            ),
            axis=(1, 3),
        )
        - 1
    ).reshape(owners, own, capacity, 1)
    to_slot = [
        ((place[None, :, 0] == ids[:, None]) | (place[None, :, 1] == ids[:, None])).astype(BF)
        for ids in block_ids
    ]
    slot_g = jnp.stack(
        [
            jnp.dot(hits, grad_low, preferred_element_type=F32)
            .astype(BF)
            .reshape(owners, capacity, width)
            for hits in to_slot
        ],
        axis=1,
    )

    inv1 = lax.rsqrt(jnp.mean(inputs * inputs, axis=-1, keepdims=True) + EPSILON)
    n1 = inputs * inv1
    normed = (n1 * attn_gain).astype(BF)
    row_start = ctx_at * rows
    query_pos = row_start + jnp.arange(rows, dtype=jnp.int32)
    inverse = 1.0 / 10000.0 ** (jnp.arange(HALF, dtype=F32) * (2.0 / HD))
    angles = inverse[:, None] * query_pos.astype(F32)[None, :]
    cos_t, sin_t = jnp.cos(angles), jnp.sin(angles)
    raw_t = jnp.einsum("dc,ld->cl", qkv_full, normed, preferred_element_type=F32)
    q_t = half_turn(raw_t[:heads_cols], cos_t, sin_t).astype(BF)
    k_t = half_turn(raw_t[heads_cols : 2 * heads_cols], cos_t, sin_t).astype(BF)
    v_t = raw_t[2 * heads_cols :].astype(BF)
    if spread:
        eout = lax.all_to_all(expert_out, "ctx", split_axis=0, concat_axis=1, tiled=True)
    else:
        eout = lax.all_gather(expert_out, "ctx", axis=1, tiled=True)
    kv_t, slot_other, slot_g, eout = tie(
        jnp.concatenate([k_t, v_t], axis=0), slot_other, slot_g, eout
    )
    before = min(ctx_count - 1, -(-(LONGEST - 1) // rows))
    shift = before * rows
    pieces = [kv_t]
    for hop in range(1, before + 1):
        links = [(i, i + hop) for i in range(ctx_count - hop)]
        pieces.insert(0, lax.ppermute(kv_t, "ctx", links))
    kv_win = jnp.concatenate(pieces, axis=1)
    k_win, v_win = kv_win[:heads_cols], kv_win[heads_cols:]

    got_g = swap(slot_g)

    starts = jnp.sum(
        seg_all[:, None] < jnp.arange(DOCS, dtype=jnp.int32)[None, :], axis=0, dtype=jnp.int32
    )
    query_seg = lax.dynamic_slice_in_dim(seg_all, row_start, rows)
    doc = jnp.sum(
        jnp.where(
            query_seg[:, None] == jnp.arange(DOCS, dtype=jnp.int32)[None, :], starts[None, :], 0
        ),
        axis=1,
    ) - (row_start - shift)
    lo = jnp.maximum(doc[::BQ], 0) // BK
    doc = doc[None, :]
    att_t, lse = attn_forward(lo, q_t, k_win, v_win, doc, shift)
    expert_in, lse, got_g = tie(expert_in, lse, got_g)
    if spread:
        ein = lax.all_to_all(expert_in, "ctx", split_axis=0, concat_axis=2, tiled=True)
    else:
        ein = lax.all_gather(expert_in, "ctx", axis=2, tiled=True)
    tensor_count = lax.axis_size("tensor")
    tensor_at = lax.axis_index("tensor")
    att_parts, out_parts = [att_t], [out_full]
    for hop in range(1, tensor_count):
        links = [(i, (i + hop) % tensor_count) for i in range(tensor_count)]
        att_parts.append(lax.ppermute(att_t, "tensor", links))
        out_parts.append(
            lax.dynamic_index_in_dim(
                out_tensor, (tensor_at - hop) % tensor_count, 0, keepdims=False
            )
        )
    branch = jnp.einsum(
        "cl,dc->ld",
        jnp.concatenate(att_parts, axis=0),
        jnp.concatenate(out_parts, axis=1),
        preferred_element_type=F32,
    )
    branch = with_layout_constraint(branch, Layout((0, 1)))
    resid = inputs + branch

    inv2 = lax.rsqrt(jnp.mean(resid * resid, axis=-1, keepdims=True) + EPSILON)
    n2 = resid * inv2
    normed2 = (n2 * ffn_gain).astype(BF)
    normed2, ein = lax.optimization_barrier((normed2, ein))

    got_x = []
    for hits in to_slot:
        sent = jnp.dot(hits, normed2, preferred_element_type=F32).astype(BF)
        if got_x:
            sent, got_x[-1] = tie(sent, got_x[-1])
        got_x.append(swap(sent.reshape(owners, 1, capacity, width)))
    shared_w = jnp.concatenate([shared_in, shared_out[None]], axis=0)
    shared_w, got_x[0] = tie(shared_w, got_x[0])
    shared_full = lax.all_gather(shared_w, DC, axis=1, tiled=True)
    router_wide = jnp.pad(router_full, ((0, 0), (0, -experts % 128)))
    ys, back_dx, g_eins, g_eouts, routers = [], [], [], [], []
    for n in range(own):
        y, dx, g_ein, g_eout, g_router = ffn(
            got_x[n],
            got_g[:, n : n + 1],
            ein[n : n + 1],
            eout[n : n + 1],
            4,
            (
                jnp.reshape(first + n, (1,)).astype(jnp.int32),
                slot_other[:, n : n + 1],
                router_wide,
            ),
        )
        ys.append(y)
        g_eins.append(g_ein)
        g_eouts.append(g_eout)
        routers.append(g_router)
        if n + 1 < own:
            dx, got_x[n + 1] = tie(dx, got_x[n + 1])
        if back_dx:
            dx, back_dx[-1] = tie(dx, back_dx[-1])
        back_dx.append(swap(dx).reshape(-1, width))
    router_part = sum(routers)[:, :experts]
    g_ein = jnp.concatenate(g_eins, axis=0)
    g_eout = jnp.concatenate(g_eouts, axis=0)

    parts = 4
    shared_shape = (parts, 1, rows // parts, width)
    sh_y, sh_dx, sh_gin, sh_gout = ffn(
        normed2.reshape(shared_shape),
        grad_low.reshape(shared_shape),
        shared_full[None, :2],
        shared_full[None, 2],
        2,
    )
    back_dx[-1], sh_dx = lax.optimization_barrier((back_dx[-1], sh_dx))

    from_slot = [
        ((place[:, 0, None] == ids[None, :]) | (place[:, 1, None] == ids[None, :])).astype(BF)
        for ids in block_ids
    ]

    def at_tokens(parts, local):
        total = local.reshape(rows, width).astype(F32)
        for hits, part in zip(from_slot, parts):
            total = total + jnp.dot(hits, part, preferred_element_type=F32)
        return total

    dn2_part = at_tokens(back_dx, sh_dx)
    dn2_low = dn2_part.astype(BF)
    ys[0], dn2_low = tie(ys[0], dn2_low)
    back_y = []
    for y in ys:
        if back_y:
            y, back_y[-1] = tie(y, back_y[-1])
        back_y.append(swap(y).reshape(-1, width))
    dn2 = lax.psum(dn2_low, "tensor")
    sh_grad, back_y[-1] = tie(jnp.concatenate([sh_gin[0], sh_gout], axis=0), back_y[-1])
    total_shared = own_sum(sh_grad, 1)
    g_eout, total_shared = tie(g_eout, total_shared)
    if spread:
        grad_eout = lax.all_to_all(g_eout, "ctx", split_axis=1, concat_axis=0, tiled=True)
    else:
        grad_eout = lax.psum_scatter(g_eout, "ctx", scatter_dimension=1, tiled=True)
    dn2, back_y[-1] = tie(dn2, back_y[-1])
    dn2 = dn2.astype(F32)
    gain2_part = jnp.sum(dn2_part * n2, axis=0)

    scaled2 = ffn_gain * dn2
    dresid = grad_layer + inv2 * (scaled2 - n2 * jnp.mean(scaled2 * n2, axis=-1, keepdims=True))
    dbranch = dresid.astype(BF)
    datt_t = jnp.einsum("dc,ld->cl", out_full, dbranch, preferred_element_type=F32).astype(BF)

    ffn_part = at_tokens(back_y, sh_y)
    ffn_low, datt_t = lax.optimization_barrier((ffn_part.astype(BF), datt_t))
    ffn_total = lax.psum(ffn_low, "tensor")

    dq_t, dk_win, dv_win = attn_backward(
        lo, q_t, k_win, v_win, att_t, datt_t, lse, doc, shift
    )
    dkv_win = jnp.concatenate([dk_win, dv_win], axis=0)
    dkv = dkv_win[:, shift:]
    for hop in range(1, before + 1):
        links = [(i + hop, i) for i in range(ctx_count - hop)]
        piece = dkv_win[:, shift - hop * rows : shift - (hop - 1) * rows]
        dkv = dkv + lax.ppermute(piece.astype(BF), "ctx", links).astype(F32)
    dq_raw = half_turn(dq_t, cos_t, -sin_t)
    dk_raw = half_turn(dkv[:heads_cols], cos_t, -sin_t)
    draw_t = jnp.concatenate([dq_raw, dk_raw, dkv[heads_cols:]], axis=0).astype(BF)
    dn1_part = jnp.einsum("cl,dc->ld", draw_t, qkv_full, preferred_element_type=F32)
    dn1_low, ffn_total = lax.optimization_barrier((dn1_part.astype(BF), ffn_total))
    layer_out = (resid + ffn_total.astype(F32)).astype(BF)
    dn1 = lax.psum(dn1_low, "tensor")
    gain1_part = jnp.sum(dn1_part * n1, axis=0)
    grad_qkv = jnp.einsum("ld,cl->dc", normed, draw_t, preferred_element_type=F32)
    grad_outw = jnp.einsum("ld,cl->dc", dbranch, att_t, preferred_element_type=F32)
    small = jnp.concatenate([router_part, gain1_part[:, None], gain2_part[:, None]], axis=1)
    mixed, grad_eout = tie(jnp.concatenate([grad_qkv, grad_outw, small], axis=1), grad_eout)
    tail = own_sum(mixed, 0)
    g_ein, tail = tie(g_ein, tail)
    small = lax.psum(tail[:, 4 * heads_cols :], "tensor")
    total_qkv = tail[:, : 3 * heads_cols].reshape(-1, 3, heads_cols).transpose(1, 0, 2)
    total_outw = tail[:, 3 * heads_cols : 4 * heads_cols]
    if spread:
        grad_ein = lax.all_to_all(g_ein, "ctx", split_axis=2, concat_axis=0, tiled=True)
    else:
        grad_ein = lax.psum_scatter(g_ein, "ctx", scatter_dimension=2, tiled=True)
    dn1, small, grad_ein = tie(dn1, small, grad_ein)
    dn1 = dn1.astype(F32)
    scaled1 = attn_gain * dn1
    grad_tokens = dresid + inv1 * (
        scaled1 - n1 * jnp.mean(scaled1 * n1, axis=-1, keepdims=True)
    )
    return (
        layer_out[None],
        grad_tokens[None],
        small[:, experts],
        total_qkv,
        total_outw,
        small[:, experts + 1],
        small[:, :experts],
        total_shared[:2],
        total_shared[2],
        grad_ein.astype(F32),
        grad_eout.astype(F32),
    )


def solution(mesh):
    return layer(mesh)


def layer(mesh):
    return jax.shard_map(
        shards,
        mesh=mesh,
        in_specs=(
            P("dp", "ctx", None),
            P("dp", None),
            P("dp", "ctx", None),
            P("dp", "ctx", None),
            P(DC),
            P(None, DC, "tensor"),
            P(DC, "tensor"),
            P(DC),
            P(DC, None),
            P(None, DC, "tensor"),
            P(DC, "tensor"),
            P("dp", None, "ctx", "tensor"),
            P("dp", "ctx", "tensor"),
            P("dp", "ctx", None),
        ),
        out_specs=(
            P("dp", "ctx", None),
            P("dp", "ctx", None),
            P(DC),
            P(None, DC, "tensor"),
            P(DC, "tensor"),
            P(DC),
            P(DC, None),
            P(None, DC, "tensor"),
            P(DC, "tensor"),
            P("dp", None, "ctx", "tensor"),
            P("dp", "ctx", "tensor"),
        ),
        check_vma=False,
    )
```

profile of v0, /device:TPU:0, one launch (start us, length us, event | category | flops | bytes accessed | tf_op | source)
XLA Modules:
  0.0 736.7 jit_solution(12734803828556731972)
XLA Ops:
  26.5 21.7 %all-gather.2 = s32[8,4,1024]{2,1,0:T(4,128)S(1)} all-gather(s32[1,4,1024]{2,1,0:T(4,128)S(1)} %add_bitcast_fusion), channel_id=2, replica_groups=mesh['dp'=2,'ctx'=4,'tensor'=4] {'dp','ctx'}, dimensions={0}, use_global_device_ids=true | all-gather | bytes 147456 | tf_op jit(solution)/shard_map/all_gather | solution.py:393
  51.1 5.3 fusion.19
  70.5 4.7 all-to-all-start.1
  84.5 50.9 %collective-permute-done = bf16[384,1024]{1,0:T(8,128)(2,1)S(1)} collective-permute-done((bf16[384,1024]{1,0:T(8,128)(2,1)S(1)}, bf16[384,1024]{1,0:T(8,128)(2,1)S(1)}, u32[]{:S(2)}, u32[]{:S(2)}) %collective-permute-start) | collective-permute-done | bytes 786464 | tf_op jit(solution)/shard_map/ppermute | solution.py:447
  138.2 8.4 %attn_fwd.1 = (bf16[192,1024]{1,0:T(8,128)(2,1)}, f32[3,1024]{1,0:T(4,128)}) custom-call(s32[2]{0:T(128)} %and_select_fusion.lo_ref, bf16[192,1024]{1,0:T(8,128)(2,1)} %bitcast.114, bf16[192,3072]{1,0:T(8,128)(2,1)} %get-tuple-element.214.k_ref, bf16[192,3072]{1,0:T(8,128)(2,1)} %get-tuple-element.213.v_ref, s32[1,1024]{1,0:T(1,128)} %bitcast.137), custom_call_target="tpu_custom_call" | custom-call | tf_op jit(solution)/shard_map/attn_fwd/pallas_call | solution.py:132
  146.7 17.4 %all-to-all-start.2 = ((bf16[8,2,192,512]{3,2,1,0:T(8,128)(2,1)}), bf16[8,2,192,512]{3,2,1,0:T(8,128)(2,1)}, u32[]{:S(2)}, u32[]{:S(2)}) async-start(bf16[8,2,192,512]{3,2,1,0:T(8,128)(2,1)} %param.25), calls=%async_computation.2 | async-start | bytes 6291456 | tf_op jit(solution)/shard_map/all_to_all | solution.py:468
  175.5 19.1 %collective-permute-done.3 = bf16[192,1024]{1,0:T(8,128)(2,1)S(1)} collective-permute-done((bf16[192,1024]{1,0:T(8,128)(2,1)S(1)}, bf16[192,1024]{1,0:T(8,128)(2,1)S(1)}, u32[]{:S(2)}, u32[]{:S(2)}) %collective-permute-start.3) | collective-permute-done | bytes 393248 | tf_op jit(solution)/shard_map/ppermute | solution.py:476
  208.8 6.2 all-to-all-start.3
  215.1 5.2 fusion.18
  220.3 19.3 %all-to-all-done.3.refs_1_ = bf16[8,1,160,768]{3,2,1,0:T(8,128)(2,1)} async-done(((bf16[8,1,160,768]{3,2,1,0:T(8,128)(2,1)}), bf16[8,1,160,768]{3,2,1,0:T(8,128)(2,1)}, u32[]{:S(2)}, u32[]{:S(2)}) %all-to-all-start.3) | async-done | bytes 1966112 | tf_op jit(solution)/shard_map/all_to_all | solution.py:380
  258.8 18.4 %ffn_experts.2 = (bf16[8,1,160,768]{3,2,1,0:T(8,128)(2,1)}, bf16[8,1,160,768]{3,2,1,0:T(8,128)(2,1)}, bf16[1,2,768,512]{3,2,1,0:T(8,128)(2,1)}, bf16[1,768,512]{2,1,0:T(8,128)(2,1)}, f32[768,128]{1,0:T(8,128)}) custom-call(s32[1]{0:T(128)} %bitcast.36.refs_0_, bf16[8,1,160,768]{3,2,1,0:T(8,128)(2,1)} %all-to-all-done.3.refs_1_, ...), custom_call_target="tpu_custom_call" | custom-call | tf_op jit(solution)/shard_map/ffn_experts/pallas_call | solution.py:263
  281.6 18.5 %ffn_experts.3 = (bf16[8,1,160,768]{3,2,1,0:T(8,128)(2,1)}, bf16[8,1,160,768]{3,2,1,0:T(8,128)(2,1)}, bf16[1,2,768,512]{3,2,1,0:T(8,128)(2,1)}, bf16[1,768,512]{2,1,0:T(8,128)(2,1)}, f32[768,128]{1,0:T(8,128)}) custom-call(s32[1]{0:T(128)} %bitcast.35.refs_0_, bf16[8,1,160,768]{3,2,1,0:T(8,128)(2,1)} %all-to-all-done.4.refs_1_, ...), custom_call_target="tpu_custom_call" | custom-call | tf_op jit(solution)/shard_map/ffn_experts/pallas_call | solution.py:263
  300.2 8.8 %all-to-all-done.5 = bf16[8,1,160,768]{3,2,1,0:T(8,128)(2,1)} async-done(((bf16[8,1,160,768]{3,2,1,0:T(8,128)(2,1)}), bf16[8,1,160,768]{3,2,1,0:T(8,128)(2,1)}, u32[]{:S(2)}, u32[]{:S(2)}) %all-to-all-start.5) | async-done | bytes 1966112 | tf_op jit(solution)/shard_map/all_to_all | solution.py:380
  308.9 4.8 all-to-all-start.6
  313.7 5.4 fusion.14
  323.8 13.1 %ffn_shared.1 = (bf16[4,1,256,768]{3,2,1,0:T(8,128)(2,1)}, bf16[4,1,256,768]{3,2,1,0:T(8,128)(2,1)}, bf16[1,2,768,512]{3,2,1,0:T(8,128)(2,1)}, bf16[1,768,512]{2,1,0:T(8,128)(2,1)}) custom-call(bf16[4,1,256,768]{3,2,1,0:T(8,128)(2,1)} %bitcast.112, bf16[4,1,256,768]{3,2,1,0:T(8,128)(2,1)} %bitcast.109, bf16[1,2,768,512]{3,2,1,0:T(8,128)(2,1)} %slice_bitcast_fusion.refs_2_, ...), custom_call_target="tpu_custom_call" | custom-call | tf_op jit(solution)/shard_map/ffn_shared/pallas_call | solution.py:263
  338.0 6.4 fusion.104
  344.4 29.4 %all_to_all.117 = bf16[8,1,160,768]{3,2,1,0:T(8,128)(2,1)} all-to-all(bf16[8,1,160,768]{3,2,1,0:T(8,128)(2,1)} %get-tuple-element.96), channel_id=1, replica_groups=mesh['dp'=2,'ctx'=4,'tensor'=4] {'dp','ctx'}, dimensions={0} | all-to-all | bytes 3932160 | tf_op jit(solution)/shard_map/all_to_all | solution.py:380
  386.0 16.5 %all-to-all-done.8 = bf16[8,1,160,768]{3,2,1,0:T(8,128)(2,1)} async-done(((bf16[8,1,160,768]{3,2,1,0:T(8,128)(2,1)}), bf16[8,1,160,768]{3,2,1,0:T(8,128)(2,1)}, u32[]{:S(2)}, u32[]{:S(2)}) %all-to-all-start.8) | async-done | bytes 1966112 | tf_op jit(solution)/shard_map/all_to_all | solution.py:380
  410.4 45.3 %all-reduce.5.cloned.1.call-done = bf16[1024,768]{1,0:T(8,128)(2,1)} async-done(((bf16[1024,768]{1,0:T(8,128)(2,1)}), bf16[1024,768]{1,0:T(8,128)(2,1)}) %all-reduce.5.cloned.1.call-update) | async-done | bytes 1572880 | tf_op jit(solution)/shard_map/psum | solution.py:563
  462.6 5.3 fusion.31
  471.7 13.5 %attn_bwd.1 = (f32[192,1024]{1,0:T(8,128)}, f32[192,3072]{1,0:T(8,128)}, f32[192,3072]{1,0:T(8,128)}) custom-call(s32[2]{0:T(128)} %and_select_fusion.lo_ref, bf16[192,1024]{1,0:T(8,128)(2,1)} %bitcast.115, bf16[192,3072]{1,0:T(8,128)(2,1)} %get-tuple-element.214.k_ref, bf16[192,3072]{1,0:T(8,128)(2,1)} %get-tuple-element.213.v_ref, ...), custom_call_target="tpu_custom_call" | custom-call | tf_op jit(solution)/shard_map/attn_bwd/pallas_call | solution.py:152
  504.9 26.6 %collective-permute-done.6 = bf16[384,1024]{1,0:T(8,128)(2,1)} collective-permute-done((bf16[384,1024]{1,0:T(8,128)(2,1)}, bf16[384,1024]{1,0:T(8,128)(2,1)}, u32[]{:S(2)}, u32[]{:S(2)}) %collective-permute-start.6) | collective-permute-done | bytes 786464 | tf_op jit(solution)/shard_map/ppermute | solution.py:592
  541.2 4.7 all-to-all-start.10
  553.2 7.6 %concatenate.47 = bf16[768,786]{0,1:T(8,128)(2,1)} concatenate(bf16[768,576]{0,1:T(8,128)(2,1)} %fusion.87, bf16[768,192]{0,1:T(8,128)(2,1)S(1)} %copy-done.24, bf16[768,16]{0,1:T(8,128)(2,1)S(1)} %copy-done.30, bf16[768,1]{0,1:T(2,128)(2,1)S(1)} %broadcast_in_dim.54, bf16[768,1]{0,1:T(2,128)(2,1)S(1)} %broadcast_in_dim.55), dimensions={1} | concatenate | bytes 2414592 | tf_op jit(solution)/shard_map/concatenate | solution.py:604
  560.8 5.1 all-to-all-done.10
  580.0 13.6 %all-to-all-done.11 = bf16[8,96,786]{2,1,0:T(8,128)(2,1)} async-done(((bf16[8,96,786]{2,1,0:T(8,128)(2,1)}), bf16[8,96,786]{2,1,0:T(8,128)(2,1)}, u32[]{:S(2)}, u32[]{:S(2)}) %all-to-all-start.11) | async-done | bytes 1207328 | tf_op jit(solution)/shard_map/all_to_all | solution.py:313
  595.2 6.8 copy.127
  602.0 4.7 all-to-all-start.12
  606.7 41.6 %all-reduce.7.cloned.1.call-done = bf16[1024,768]{1,0:T(8,128)(2,1)} async-done(((bf16[1024,768]{1,0:T(8,128)(2,1)}), bf16[1024,768]{1,0:T(8,128)(2,1)}) %all-reduce.7.cloned.1.call-update) | async-done | bytes 1572880 | tf_op jit(solution)/shard_map/psum | solution.py:582
  656.7 19.9 %psum.31 = f32[96,18]{1,0:T(8,128)S(1)} all-reduce(f32[96,18]{1,0:T(8,128)S(1)} %slice.200), channel_id=1, replica_groups=mesh['dp'=2,'ctx'=4,'tensor'=4] {'tensor'}, use_global_device_ids=true, to_apply=%region_14.15 | all-reduce | flops 1728 | bytes 13824 | tf_op jit(solution)/shard_map/psum | solution.py:607
  679.3 41.0 %all-reduce.9.cloned.1.call-done = bf16[1024,768]{1,0:T(8,128)(2,1)} async-done(((bf16[1024,768]{1,0:T(8,128)(2,1)}), bf16[1024,768]{1,0:T(8,128)(2,1)}) %all-reduce.9.cloned.1.call-update) | async-done | bytes 1572880 | tf_op jit(solution)/shard_map/psum | solution.py:599
  (255 shorter events, 206.3 us)
Async XLA Ops:
  7.2 58.8 %all-gather.7.cloned.1.call-start = ((), (), s32[]{:S(2)}) async-start(), calls=%async_computation.13 | async-start | bytes 1548288 | tf_op jit(solution)/shard_map/all_gather | solution.py:364
  12.4 50.8 %all-to-all-start = ((bf16[8,192,512]{2,1,0:T(8,128)(2,1)}), bf16[8,192,512]{2,1,0:T(8,128)(2,1)}, u32[]{:S(2)}, u32[]{:S(2)}) async-start(bf16[8,192,512]{2,1,0:T(8,128)(2,1)} %param.26), calls=%async_computation | async-start | bytes 3145728 | tf_op jit(solution)/shard_map/all_to_all | solution.py:436
  24.9 25.7 %copy-start.3 = (bf16[1,1024,768]{2,1,0:T(8,128)(2,1)S(1)}, bf16[1,1024,768]{2,1,0:T(8,128)(2,1)}, u32[]{:S(2)}) copy-start(bf16[1,1024,768]{2,1,0:T(8,128)(2,1)} %param.14) | copy-start | bytes 4718596
  26.0 31.2 %copy-start.35 = (s32[1024]{0:T(1024)}, s32[1024]{0:T(1024)S(1)}, u32[]{:S(2)}) copy-start(s32[1024]{0:T(1024)S(1)} %get-tuple-element.199) | copy-start | bytes 12292
  26.0 31.2 %copy-start.37 = (s32[1024]{0:T(1024)}, s32[1024]{0:T(1024)S(1)}, u32[]{:S(2)}) copy-start(s32[1024]{0:T(1024)S(1)} %get-tuple-element.200) | copy-start | bytes 12292
  70.5 76.2 %all-to-all-start.1 = ((bf16[8,2,160,768]{3,2,1,0:T(8,128)(2,1)}), bf16[8,2,160,768]{3,2,1,0:T(8,128)(2,1)}, u32[]{:S(2)}, u32[]{:S(2)}) async-start(bf16[8,2,160,768]{3,2,1,0:T(8,128)(2,1)} %pad_maximum_fusion), calls=%async_computation.1 | async-start | bytes 7864320 | tf_op jit(solution)/shard_map/all_to_all | solution.py:380
  75.2 94.4 %all-gather.11.cloned.1.call-start = ((), (), s32[]{:S(2)}) async-start(), calls=%async_computation.18 | async-start | bytes 1966080 | tf_op jit(solution)/shard_map/all_gather | solution.py:367
  75.4 60.0 %collective-permute-start = (bf16[384,1024]{1,0:T(8,128)(2,1)S(1)}, bf16[384,1024]{1,0:T(8,128)(2,1)S(1)}, u32[]{:S(2)}, u32[]{:S(2)}) collective-permute-start(bf16[384,1024]{1,0:T(8,128)(2,1)S(1)} %pad_maximum_fusion.5), channel_id=1, source_target_pairs={{0,8},{4,12},{1,9},{5,13},{2,10},{6,14},{3,11},{7,15},{16,24},{20,... | collective-permute-start | bytes 2359304 | tf_op jit(solution)/shard_map/ppermute | solution.py:447
  79.2 56.2 %collective-permute-start.1 = (bf16[384,1024]{1,0:T(8,128)(2,1)S(1)}, bf16[384,1024]{1,0:T(8,128)(2,1)}, u32[]{:S(2)}, u32[]{:S(2)}) collective-permute-start(bf16[384,1024]{1,0:T(8,128)(2,1)S(1)} %pad_maximum_fusion.5), channel_id=1, source_target_pairs={{0,4},{4,8},{8,12},{1,5},{5,9},{9,13},{2,6},{6,10},{10,14},{3,7},{... | collective-permute-start | bytes 2359304 | tf_op jit(solution)/shard_map/ppermute | solution.py:447
  82.1 54.5 %copy-start.33 = (s32[1024]{0:T(1024)}, s32[1024]{0:T(1024)S(1)}, u32[]{:S(2)}) copy-start(s32[1024]{0:T(1024)S(1)} %broadcast_subtract_fusion) | copy-start | bytes 12292
  146.7 54.4 %all-to-all-start.2 = ((bf16[8,2,192,512]{3,2,1,0:T(8,128)(2,1)}), bf16[8,2,192,512]{3,2,1,0:T(8,128)(2,1)}, u32[]{:S(2)}, u32[]{:S(2)}) async-start(bf16[8,2,192,512]{3,2,1,0:T(8,128)(2,1)} %param.25), calls=%async_computation.2 | async-start | bytes 6291456 | tf_op jit(solution)/shard_map/all_to_all | solution.py:468
  164.1 11.5 %collective-permute-start.2 = (bf16[192,1024]{1,0:T(8,128)(2,1)S(1)}, bf16[192,1024]{1,0:T(8,128)(2,1)S(1)}, u32[]{:S(2)}, u32[]{:S(2)}) collective-permute-start(bf16[192,1024]{1,0:T(8,128)(2,1)S(1)} %copy-done.18), channel_id=1, source_target_pairs={{0,1},{1,2},{2,3},{3,0},{4,5},{5,6},{6,7},{7,4},{8,9},{9,10},{10,1... | collective-permute-start | bytes 1179656 | tf_op jit(solution)/shard_map/ppermute | solution.py:476
  165.6 29.0 %collective-permute-start.3 = (bf16[192,1024]{1,0:T(8,128)(2,1)S(1)}, bf16[192,1024]{1,0:T(8,128)(2,1)S(1)}, u32[]{:S(2)}, u32[]{:S(2)}) collective-permute-start(bf16[192,1024]{1,0:T(8,128)(2,1)S(1)} %copy-done.18), channel_id=1, source_target_pairs={{0,2},{1,3},{2,0},{3,1},{4,6},{5,7},{6,4},{7,5},{8,10},{9,11},{10,... | collective-permute-start | bytes 1179656 | tf_op jit(solution)/shard_map/ppermute | solution.py:476
  168.2 26.4 %collective-permute-start.4 = (bf16[192,1024]{1,0:T(8,128)(2,1)S(1)}, bf16[192,1024]{1,0:T(8,128)(2,1)S(1)}, u32[]{:S(2)}, u32[]{:S(2)}) collective-permute-start(bf16[192,1024]{1,0:T(8,128)(2,1)S(1)} %copy-done.18), channel_id=1, source_target_pairs={{0,3},{1,0},{2,1},{3,2},{4,7},{5,4},{6,5},{7,6},{8,11},{9,8},{10,9... | collective-permute-start | bytes 1179656 | tf_op jit(solution)/shard_map/ppermute | solution.py:476
  175.5 19.1 %copy-start.45 = (bf16[192,1024]{1,0:T(8,128)(2,1)}, bf16[192,1024]{1,0:T(8,128)(2,1)S(1)}, u32[]{:S(2)}) copy-start(bf16[192,1024]{1,0:T(8,128)(2,1)S(1)} %collective-permute-done.2) | copy-start | bytes 1179652
  208.8 30.8 %all-to-all-start.3 = ((bf16[8,1,160,768]{3,2,1,0:T(8,128)(2,1)}), bf16[8,1,160,768]{3,2,1,0:T(8,128)(2,1)}, u32[]{:S(2)}, u32[]{:S(2)}) async-start(bf16[8,1,160,768]{3,2,1,0:T(8,128)(2,1)} %bitcast.121), calls=%async_computation.3 | async-start | bytes 3932160 | tf_op jit(solution)/shard_map/all_to_all | solution.py:380
  220.3 24.0 %copy-start.29 = (bf16[2,96,512]{2,1,0:T(8,128)(2,1)S(1)}, bf16[2,96,512]{2,1,0:T(8,128)(2,1)}, u32[]{:S(2)}) copy-start(bf16[2,96,512]{2,1,0:T(8,128)(2,1)} %param.23) | copy-start | bytes 589828
  220.3 24.0 %copy-start.31 = (bf16[96,512]{1,0:T(8,128)(2,1)S(1)}, bf16[96,512]{1,0:T(8,128)(2,1)}, u32[]{:S(2)}) copy-start(bf16[96,512]{1,0:T(8,128)(2,1)} %param.24) | copy-start | bytes 294916
  239.6 37.6 %all-to-all-start.4 = ((bf16[8,1,160,768]{3,2,1,0:T(8,128)(2,1)}), bf16[8,1,160,768]{3,2,1,0:T(8,128)(2,1)}, u32[]{:S(2)}, u32[]{:S(2)}) async-start(bf16[8,1,160,768]{3,2,1,0:T(8,128)(2,1)} %bitcast.119), calls=%async_computation.4 | async-start | bytes 3932160 | tf_op jit(solution)/shard_map/all_to_all | solution.py:380
  244.0 75.1 %all-gather.9.cloned.1.call-start = ((), (), s32[]{:S(2)}) async-start(), calls=%async_computation.14 | async-start | bytes 2654208 | tf_op jit(solution)/shard_map/all_gather | solution.py:504
  277.3 31.7 %all-to-all-start.5 = ((bf16[8,1,160,768]{3,2,1,0:T(8,128)(2,1)}), bf16[8,1,160,768]{3,2,1,0:T(8,128)(2,1)}, u32[]{:S(2)}, u32[]{:S(2)}) async-start(bf16[8,1,160,768]{3,2,1,0:T(8,128)(2,1)} %get-tuple-element.90), calls=%async_computation.5 | async-start | bytes 3932160 | tf_op jit(solution)/shard_map/all_to_all | solution.py:380
  308.9 29.1 %all-to-all-start.6 = ((bf16[8,1,160,768]{3,2,1,0:T(8,128)(2,1)}), bf16[8,1,160,768]{3,2,1,0:T(8,128)(2,1)}, u32[]{:S(2)}, u32[]{:S(2)}) async-start(bf16[8,1,160,768]{3,2,1,0:T(8,128)(2,1)} %get-tuple-element.91), calls=%async_computation.6 | async-start | bytes 3932160 | tf_op jit(solution)/shard_map/all_to_all | solution.py:380
  373.8 28.6 %all-to-all-start.8 = ((bf16[8,1,160,768]{3,2,1,0:T(8,128)(2,1)}), bf16[8,1,160,768]{3,2,1,0:T(8,128)(2,1)}, u32[]{:S(2)}, u32[]{:S(2)}) async-start(bf16[8,1,160,768]{3,2,1,0:T(8,128)(2,1)} %get-tuple-element.101), calls=%async_computation.8 | async-start | bytes 3932160 | tf_op jit(solution)/shard_map/all_to_all | solution.py:380
  378.1 77.6 %all-reduce.5.cloned.1.call-start = ((), (), s32[]{:S(2)}) async-start(), calls=%async_computation.15 | async-start | bytes 3145728 | tf_op jit(solution)/shard_map/psum | solution.py:563
  405.8 129.6 %all-to-all-start.9 = ((bf16[3,8,96,512]{3,2,0,1:T(8,128)(2,1)}), bf16[3,8,96,512]{3,2,0,1:T(8,128)(2,1)}, u32[]{:S(2)}, u32[]{:S(2)}) async-start(bf16[3,8,96,512]{3,2,0,1:T(8,128)(2,1)} %copy.123), calls=%async_computation.9 | async-start | bytes 4718592 | tf_op jit(solution)/shard_map/all_to_all | solution.py:313
  491.1 13.7 %collective-permute-start.5 = (bf16[384,1024]{1,0:T(8,128)(2,1)}, bf16[384,1024]{1,0:T(8,128)(2,1)}, u32[]{:S(2)}, u32[]{:S(2)}) collective-permute-start(bf16[384,1024]{1,0:T(8,128)(2,1)} %get-tuple-element.211), channel_id=1, source_target_pairs={{4,0},{8,4},{12,8},{5,1},{9,5},{13,9},{6,2},{10,6},{14,10},{7,3},{... | collective-permute-start | bytes 2359304 | tf_op jit(solution)/shard_map/ppermute | solution.py:592
  492.6 38.9 %collective-permute-start.6 = (bf16[384,1024]{1,0:T(8,128)(2,1)}, bf16[384,1024]{1,0:T(8,128)(2,1)}, u32[]{:S(2)}, u32[]{:S(2)}) collective-permute-start(bf16[384,1024]{1,0:T(8,128)(2,1)} %get-tuple-element.212), channel_id=1, source_target_pairs={{8,0},{12,4},{9,1},{13,5},{10,2},{14,6},{11,3},{15,7},{24,16},{28,... | collective-permute-start | bytes 2359304 | tf_op jit(solution)/shard_map/ppermute | solution.py:592
  541.2 24.8 %all-to-all-start.10 = ((bf16[2,768,512]{2,0,1:T(2,128)(2,1)}), bf16[2,768,512]{2,0,1:T(2,128)(2,1)}, u32[]{:S(2)}, u32[]{:S(2)}) async-start(bf16[2,768,512]{2,0,1:T(2,128)(2,1)} %copy.124), calls=%async_computation.10 | async-start | bytes 3145728 | tf_op jit(solution)/shard_map/all_to_all | solution.py:568
  571.3 22.3 %all-to-all-start.11 = ((bf16[8,96,786]{2,1,0:T(8,128)(2,1)}), bf16[8,96,786]{2,1,0:T(8,128)(2,1)}, u32[]{:S(2)}, u32[]{:S(2)}) async-start(bf16[8,96,786]{2,1,0:T(8,128)(2,1)} %bitcast.113), calls=%async_computation.11 | async-start | bytes 2752512 | tf_op jit(solution)/shard_map/all_to_all | solution.py:313
  575.6 72.7 %all-reduce.7.cloned.1.call-start = ((), (), s32[]{:S(2)}) async-start(), calls=%async_computation.16 | async-start | bytes 3145728 | tf_op jit(solution)/shard_map/psum | solution.py:582
  602.0 74.7 %all-to-all-start.12 = ((bf16[2,2,768,512]{3,1,0,2:T(2,128)(2,1)}), bf16[2,2,768,512]{3,1,0,2:T(2,128)(2,1)}, u32[]{:S(2)}, u32[]{:S(2)}) async-start(bf16[2,2,768,512]{3,1,0,2:T(2,128)(2,1)} %copy.127), calls=%async_computation.12 | async-start | bytes 6291456 | tf_op jit(solution)/shard_map/all_to_all | solution.py:611
  606.6 113.6 %all-reduce.9.cloned.1.call-start = ((), (), s32[]{:S(2)}) async-start(), calls=%async_computation.17 | async-start | bytes 3145728 | tf_op jit(solution)/shard_map/psum | solution.py:599
  (44 other events, 189.6 us)
Sparse Core Ops, SparseCore 0:
  12.5 32.4 all-gather.6
  83.8 37.3 all-gather.10
  247.3 46.9 all-gather.8
  381.6 74.0 all-reduce.4
  579.0 69.1 all-reduce.6
  650.5 69.7 all-reduce.8
where the time goes:
time: 746 us; the launch traced here: 737 us
  waiting for transfers between devices  299 us (40%)
  local copies, waits for them, and re-layouts  84 us (11%)
  starting transfers between devices  84 us (11%)
  Pallas kernels  71.9 us (10%)
  blocking collectives  71 us (10%)
  matrix products  61.6 us (8%)
  other arithmetic  49.5 us (7%)
  between operations  15.3 us (2%)
    ppermute x2, waiting for transfers between devices, shards(): pieces.insert(0, lax.ppermute(kv_t, 'ctx', links))  50.9 us
    pallas_call x3, Pallas kernels, ffn(): pl.pallas_call(functools.partial(ffn_kernel, gated=gated), out_shape=outs...  50 us
    all_to_all x6, waiting for transfers between devices, swap(): lax.all_to_all(values, expert_axes, split_axis=0, concat_axis=0, tiled=True)  45.7 us
    psum x1, waiting for transfers between devices, shards(): dn2 = lax.psum(dn2_low, 'tensor')  45.3 us
    psum x1, waiting for transfers between devices, shards(): ffn_total = lax.psum(ffn_low, 'tensor')  41.6 us
    psum x1, waiting for transfers between devices, shards(): dn1 = lax.psum(dn1_low, 'tensor')  41 us
    ppermute x2, waiting for transfers between devices, shards(): dkv = dkv + lax.ppermute(piece.astype(BF), 'ctx', links).astype(F32)  31.2 us
    all_to_all x1, blocking collectives, swap(): lax.all_to_all(values, expert_axes, split_axis=0, concat_axis=0, tiled=True)  29.4 us
  transfers between devices with their start and end apart: 25, of which 15 were waited for; matrix products, arithmetic and copies ran while one was open for 20% of the time, Pallas kernels for 10%

commit v1 on v0

--- a/solution.py
+++ b/solution.py
@@ -233,17 +233,20 @@
             grouter_ref[...] = acc_router[...]
 
 
-def ffn(x, g, w_in, w_out, block, routing=None):
+def ffn(x, g, w_in, w_out, block, routing=None, at=0):
     sources, experts, rows, width = x.shape
     units = w_out.shape[2]
     gated = routing is not None
     block = math.gcd(sources, block)
     big = pl.BlockSpec((block, 1, rows, width), lambda e, s, *_: (s, e, 0, 0))
+    big_at = pl.BlockSpec((block, 1, rows, width), lambda e, s, *_: (s, at + e, 0, 0))
+    w_in_at = pl.BlockSpec((1, 2, width, units), lambda e, s, *_: (at + e, 0, 0, 0))
+    w_out_at = pl.BlockSpec((1, width, units), lambda e, s, *_: (at + e, 0, 0))
     w_in_spec = pl.BlockSpec((1, 2, width, units), lambda e, s, *_: (e, 0, 0, 0))
     w_out_spec = pl.BlockSpec((1, width, units), lambda e, s, *_: (e, 0, 0))
     wide = jax.ShapeDtypeStruct(x.shape, BF)
     ins = [x, g]
-    in_specs = [big, big]
+    in_specs = [big, big_at]
     outs = [
         wide,
         wide,
@@ -256,7 +259,8 @@
         first, other, router = routing
         router_spec = pl.BlockSpec(router.shape, lambda e, s, *_: (0, 0))
         ins = [first] + ins + [other, router]
-        in_specs += [pl.BlockSpec((block, 1, rows, 1), lambda e, s, *_: (s, e, 0, 0)), router_spec]
+        thin = pl.BlockSpec((block, 1, rows, 1), lambda e, s, *_: (s, at + e, 0, 0))
+        in_specs += [thin, router_spec]
         outs.append(jax.ShapeDtypeStruct(router.shape, F32))
         out_specs.append(router_spec)
         scratch.append(pltpu.VMEM(router.shape, F32))
@@ -266,7 +270,7 @@
         grid_spec=pltpu.PrefetchScalarGridSpec(
             num_scalar_prefetch=1 if gated else 0,
             grid=(experts, sources // block),
-            in_specs=in_specs + [w_in_spec, w_out_spec],
+            in_specs=in_specs + [w_in_at, w_out_at],
             out_specs=out_specs,
             scratch_shapes=scratch,
         ),
@@ -436,9 +440,7 @@
         eout = lax.all_to_all(expert_out, "ctx", split_axis=0, concat_axis=1, tiled=True)
     else:
         eout = lax.all_gather(expert_out, "ctx", axis=1, tiled=True)
-    kv_t, slot_other, slot_g, eout = tie(
-        jnp.concatenate([k_t, v_t], axis=0), slot_other, slot_g, eout
-    )
+    kv_t, slot_other, eout = tie(jnp.concatenate([k_t, v_t], axis=0), slot_other, eout)
     before = min(ctx_count - 1, -(-(LONGEST - 1) // rows))
     shift = before * rows
     pieces = [kv_t]
@@ -446,6 +448,7 @@
         links = [(i, i + hop) for i in range(ctx_count - hop)]
         pieces.insert(0, lax.ppermute(kv_t, "ctx", links))
     kv_win = jnp.concatenate(pieces, axis=1)
+    kv_win, slot_g = tie(kv_win, slot_g)
     k_win, v_win = kv_win[:heads_cols], kv_win[heads_cols:]
 
     got_g = swap(slot_g)
@@ -507,15 +510,12 @@
     for n in range(own):
         y, dx, g_ein, g_eout, g_router = ffn(
             got_x[n],
-            got_g[:, n : n + 1],
-            ein[n : n + 1],
-            eout[n : n + 1],
+            got_g,
+            ein,
+            eout,
             4,
-            (
-                jnp.reshape(first + n, (1,)).astype(jnp.int32),
-                slot_other[:, n : n + 1],
-                router_wide,
-            ),
+            (jnp.reshape(first + n, (1,)).astype(jnp.int32), slot_other, router_wide),
+            n,
         )
         ys.append(y)
         g_eins.append(g_ein)
@@ -563,11 +563,6 @@
     dn2 = lax.psum(dn2_low, "tensor")
     sh_grad, back_y[-1] = tie(jnp.concatenate([sh_gin[0], sh_gout], axis=0), back_y[-1])
     total_shared = own_sum(sh_grad, 1)
-    g_eout, total_shared = tie(g_eout, total_shared)
-    if spread:
-        grad_eout = lax.all_to_all(g_eout, "ctx", split_axis=1, concat_axis=0, tiled=True)
-    else:
-        grad_eout = lax.psum_scatter(g_eout, "ctx", scatter_dimension=1, tiled=True)
     dn2, back_y[-1] = tie(dn2, back_y[-1])
     dn2 = dn2.astype(F32)
     gain2_part = jnp.sum(dn2_part * n2, axis=0)
@@ -593,6 +588,11 @@
     dq_raw = half_turn(dq_t, cos_t, -sin_t)
     dk_raw = half_turn(dkv[:heads_cols], cos_t, -sin_t)
     draw_t = jnp.concatenate([dq_raw, dk_raw, dkv[heads_cols:]], axis=0).astype(BF)
+    g_eout, draw_t, total_shared = tie(g_eout, draw_t, total_shared)
+    if spread:
+        grad_eout = lax.all_to_all(g_eout, "ctx", split_axis=1, concat_axis=0, tiled=True)
+    else:
+        grad_eout = lax.psum_scatter(g_eout, "ctx", scatter_dimension=1, tiled=True)
     dn1_part = jnp.einsum("cl,dc->ld", draw_t, qkv_full, preferred_element_type=F32)
     dn1_low, ffn_total = lax.optimization_barrier((dn1_part.astype(BF), ffn_total))
     layer_out = (resid + ffn_total.astype(F32)).astype(BF)

time: 746 us -> 751 us (level)
  other arithmetic: 49.5 us -> 60 us
  local copies, waits for them, and re-layouts: 84 us -> 75.6 us
    ppermute x2, waiting for transfers between devices: 50.9 us -> 7.45 us  [shards(): pieces.insert(0, lax.ppermute(kv_t, 'ctx', links))]
    all_to_all x6, waiting for transfers between devices: 45.7 us -> 79.2 us  [swap(): lax.all_to_all(values, expert_axes, split_axis=0, concat_axis=0, tiled=True)]
    all_to_all x1, starting transfers between devices: 17.4 us -> 4.8 us  [shards(): lax.all_to_all(expert_in, 'ctx', split_axis=0, concat_axis=2, tiled=True)]
    slice x4 -> x0, local copies, waits for them, and re-layouts: 11.5 us -> none  [the longest x1 4.46 us: shards(): got_g[:, n:n + 1]]
    all_to_all x2, starting transfers between devices: 8.81 us -> 19.5 us  [own_sum(): lax.all_to_all(parts.astype(BF).reshape(cut), DC, split_axis=axis, concat...]
    ppermute x3, waiting for transfers between devices: 23.8 us -> 31.8 us  [shards(): att_parts.append(lax.ppermute(att_t, 'tensor', links))]
  transfers between devices with their start and end apart: 25 -> 25, of which waited for: 15 -> 14; matrix products, arithmetic and copies ran while one was open for 20% -> 17% of each run, Pallas kernels for 10% -> 8%
where the time goes in v1:
time: 751 us; the launch traced here: 742 us
  waiting for transfers between devices  295 us (39%)
  starting transfers between devices  90.3 us (12%)
  local copies, waits for them, and re-layouts  75.6 us (10%)
  Pallas kernels  71.6 us (10%)
  blocking collectives  70.8 us (9%)
  matrix products  63.5 us (8%)
  other arithmetic  60 us (8%)
  between operations  15.1 us (2%)
    all_to_all x6, waiting for transfers between devices, swap(): lax.all_to_all(values, expert_axes, split_axis=0, concat_axis=0, tiled=True)  79.2 us
    pallas_call x3, Pallas kernels, ffn(): pl.pallas_call(functools.partial(ffn_kernel, gated=gated), out_shape=outs...  49.8 us
    psum x1, waiting for transfers between devices, shards(): dn2 = lax.psum(dn2_low, 'tensor')  48.5 us
    psum x1, waiting for transfers between devices, shards(): ffn_total = lax.psum(ffn_low, 'tensor')  41 us
    psum x1, waiting for transfers between devices, shards(): dn1 = lax.psum(dn1_low, 'tensor')  37.7 us
    ppermute x2, waiting for transfers between devices, shards(): dkv = dkv + lax.ppermute(piece.astype(BF), 'ctx', links).astype(F32)  34.7 us
    all_to_all x6, starting transfers between devices, swap(): lax.all_to_all(values, expert_axes, split_axis=0, concat_axis=0, tiled=True)  32.6 us
    ppermute x3, waiting for transfers between devices, shards(): att_parts.append(lax.ppermute(att_t, 'tensor', links))  31.8 us
  transfers between devices with their start and end apart: 25, of which 14 were waited for; matrix products, arithmetic and copies ran while one was open for 17% of the time, Pallas kernels for 8%

profile of v1, /device:TPU:0, one launch (start us, length us, event | category | flops | bytes accessed | tf_op | source)
XLA Modules:
  0.0 741.6 jit_solution(3781627000399375213)
XLA Ops:
  26.5 21.7 %all-gather.2 = s32[8,4,1024]{2,1,0:T(4,128)S(1)} all-gather(s32[1,4,1024]{2,1,0:T(4,128)S(1)} %add_bitcast_fusion), channel_id=2, replica_groups=mesh['dp'=2,'ctx'=4,'tensor'=4] {'dp','ctx'}, dimensions={0}, use_global_device_ids=true | all-gather | bytes 147456 | tf_op jit(solution)/shard_map/all_gather | solution.py:397
  76.5 7.4 %collective-permute-done = bf16[384,1024]{1,0:T(8,128)(2,1)} collective-permute-done((bf16[384,1024]{1,0:T(8,128)(2,1)S(1)}, bf16[384,1024]{1,0:T(8,128)(2,1)}, u32[]{:S(2)}, u32[]{:S(2)}) %collective-permute-start) | collective-permute-done | bytes 786464 | tf_op jit(solution)/shard_map/ppermute | solution.py:449
  85.5 10.3 %all-to-all-start.1 = ((bf16[8,2,160,768]{3,2,1,0:T(8,128)(2,1)}), bf16[8,2,160,768]{3,2,1,0:T(8,128)(2,1)}, u32[]{:S(2)}, u32[]{:S(2)}) async-start(bf16[8,2,160,768]{3,2,1,0:T(8,128)(2,1)} %pad_maximum_fusion), calls=%async_computation.1 | async-start | bytes 7864320 | tf_op jit(solution)/shard_map/all_to_all | solution.py:384
  101.3 8.4 %attn_fwd.1 = (bf16[192,1024]{1,0:T(8,128)(2,1)}, f32[3,1024]{1,0:T(4,128)}) custom-call(s32[2]{0:T(128)} %and_select_fusion.lo_ref, bf16[192,1024]{1,0:T(8,128)(2,1)} %bitcast.118, bf16[192,3072]{1,0:T(8,128)(2,1)} %get-tuple-element.214.k_ref, bf16[192,3072]{1,0:T(8,128)(2,1)} %get-tuple-element.213.v_ref, s32[1,1024]{1,0:T(1,128)} %bitcast.139), custom_call_target="tpu_custom_call" | custom-call | tf_op jit(solution)/shard_map/attn_fwd/pallas_call | solution.py:132
  109.7 31.8 %all-to-all-done.1.refs_2_ = bf16[8,2,160,768]{3,2,1,0:T(8,128)(2,1)} async-done(((bf16[8,2,160,768]{3,2,1,0:T(8,128)(2,1)}), bf16[8,2,160,768]{3,2,1,0:T(8,128)(2,1)}, u32[]{:S(2)}, u32[]{:S(2)}) %all-to-all-start.1) | async-done | bytes 3932192 | tf_op jit(solution)/shard_map/all_to_all | solution.py:384
  141.5 4.8 all-to-all-start.2
  152.5 7.3 collective-permute-done.4
  159.8 24.5 %collective-permute-done.3 = bf16[192,1024]{1,0:T(8,128)(2,1)S(1)} collective-permute-done((bf16[192,1024]{1,0:T(8,128)(2,1)S(1)}, bf16[192,1024]{1,0:T(8,128)(2,1)S(1)}, u32[]{:S(2)}, u32[]{:S(2)}) %collective-permute-start.3) | collective-permute-done | bytes 393248 | tf_op jit(solution)/shard_map/ppermute | solution.py:479
  202.8 5.2 fusion.18
  208.0 19.1 %all-to-all-done.3.refs_1_ = bf16[8,1,160,768]{3,2,1,0:T(8,128)(2,1)} async-done(((bf16[8,1,160,768]{3,2,1,0:T(8,128)(2,1)}), bf16[8,1,160,768]{3,2,1,0:T(8,128)(2,1)}, u32[]{:S(2)}, u32[]{:S(2)}) %all-to-all-start.3) | async-done | bytes 1966112 | tf_op jit(solution)/shard_map/all_to_all | solution.py:384
  236.7 18.3 %ffn_experts.2 = (bf16[8,1,160,768]{3,2,1,0:T(8,128)(2,1)}, bf16[8,1,160,768]{3,2,1,0:T(8,128)(2,1)}, bf16[1,2,768,512]{3,2,1,0:T(8,128)(2,1)}, bf16[1,768,512]{2,1,0:T(8,128)(2,1)}, f32[768,128]{1,0:T(8,128)}) custom-call(s32[1]{0:T(128)} %bitcast.26.refs_0_, bf16[8,1,160,768]{3,2,1,0:T(8,128)(2,1)} %all-to-all-done.3.refs_1_, ...), custom_call_target="tpu_custom_call" | custom-call | tf_op jit(solution)/shard_map/ffn_experts/pallas_call | solution.py:267
  263.6 18.2 %ffn_experts.3 = (bf16[8,1,160,768]{3,2,1,0:T(8,128)(2,1)}, bf16[8,1,160,768]{3,2,1,0:T(8,128)(2,1)}, bf16[1,2,768,512]{3,2,1,0:T(8,128)(2,1)}, bf16[1,768,512]{2,1,0:T(8,128)(2,1)}, f32[768,128]{1,0:T(8,128)}) custom-call(s32[1]{0:T(128)} %bitcast.32.refs_0_, bf16[8,1,160,768]{3,2,1,0:T(8,128)(2,1)} %all-to-all-done.4.refs_1_, ...), custom_call_target="tpu_custom_call" | custom-call | tf_op jit(solution)/shard_map/ffn_experts/pallas_call | solution.py:267
  281.9 6.9 all-to-all-done.5
  293.3 5.4 fusion.14
  303.5 13.2 %ffn_shared.1 = (bf16[4,1,256,768]{3,2,1,0:T(8,128)(2,1)}, bf16[4,1,256,768]{3,2,1,0:T(8,128)(2,1)}, bf16[1,2,768,512]{3,2,1,0:T(8,128)(2,1)}, bf16[1,768,512]{2,1,0:T(8,128)(2,1)}) custom-call(bf16[4,1,256,768]{3,2,1,0:T(8,128)(2,1)} %bitcast.116, bf16[4,1,256,768]{3,2,1,0:T(8,128)(2,1)} %bitcast.114, bf16[1,2,768,512]{3,2,1,0:T(8,128)(2,1)} %slice_bitcast_fusion.refs_2_, ...), custom_call_target="tpu_custom_call" | custom-call | tf_op jit(solution)/shard_map/ffn_shared/pallas_call | solution.py:267
  317.6 6.4 fusion.98
  324.0 29.4 %all_to_all.117 = bf16[8,1,160,768]{3,2,1,0:T(8,128)(2,1)} all-to-all(bf16[8,1,160,768]{3,2,1,0:T(8,128)(2,1)} %get-tuple-element.101), channel_id=1, replica_groups=mesh['dp'=2,'ctx'=4,'tensor'=4] {'dp','ctx'}, dimensions={0} | all-to-all | bytes 3932160 | tf_op jit(solution)/shard_map/all_to_all | solution.py:384
  365.6 16.5 %all-to-all-done.8 = bf16[8,1,160,768]{3,2,1,0:T(8,128)(2,1)} async-done(((bf16[8,1,160,768]{3,2,1,0:T(8,128)(2,1)}), bf16[8,1,160,768]{3,2,1,0:T(8,128)(2,1)}, u32[]{:S(2)}, u32[]{:S(2)}) %all-to-all-start.8) | async-done | bytes 1966112 | tf_op jit(solution)/shard_map/all_to_all | solution.py:384
  382.1 48.5 %all-reduce.5.cloned.1.call-done = bf16[1024,768]{1,0:T(8,128)(2,1)} async-done(((bf16[1024,768]{1,0:T(8,128)(2,1)}), bf16[1024,768]{1,0:T(8,128)(2,1)}) %all-reduce.5.cloned.1.call-update) | async-done | bytes 1572880 | tf_op jit(solution)/shard_map/psum | solution.py:563
  438.1 5.2 fusion.31
  447.1 13.4 %attn_bwd.1 = (f32[192,1024]{1,0:T(8,128)}, f32[192,3072]{1,0:T(8,128)}, f32[192,3072]{1,0:T(8,128)}) custom-call(s32[2]{0:T(128)} %and_select_fusion.lo_ref, bf16[192,1024]{1,0:T(8,128)(2,1)} %bitcast.119, bf16[192,3072]{1,0:T(8,128)(2,1)} %get-tuple-element.214.k_ref, bf16[192,3072]{1,0:T(8,128)(2,1)} %get-tuple-element.213.v_ref, ...), custom_call_target="tpu_custom_call" | custom-call | tf_op jit(solution)/shard_map/attn_bwd/pallas_call | solution.py:152
  465.5 14.1 %all-to-all-start.9 = ((bf16[3,8,96,512]{3,2,0,1:T(8,128)(2,1)}), bf16[3,8,96,512]{3,2,0,1:T(8,128)(2,1)}, u32[]{:S(2)}, u32[]{:S(2)}) async-start(bf16[3,8,96,512]{3,2,0,1:T(8,128)(2,1)} %copy.122), calls=%async_computation.9 | async-start | bytes 4718592 | tf_op jit(solution)/shard_map/all_to_all | solution.py:317
  490.2 34.7 %collective-permute-done.6 = bf16[384,1024]{1,0:T(8,128)(2,1)S(1)} collective-permute-done((bf16[384,1024]{1,0:T(8,128)(2,1)S(1)}, bf16[384,1024]{1,0:T(8,128)(2,1)S(1)}, u32[]{:S(2)}, u32[]{:S(2)}) %collective-permute-start.6) | collective-permute-done | bytes 786464 | tf_op jit(solution)/shard_map/ppermute | solution.py:587
  535.1 9.6 %all-to-all-start.10 = ((bf16[2,768,512]{2,0,1:T(2,128)(2,1)}), bf16[2,768,512]{2,0,1:T(2,128)(2,1)}, u32[]{:S(2)}, u32[]{:S(2)}) async-start(bf16[2,768,512]{2,0,1:T(2,128)(2,1)} %copy.124), calls=%async_computation.10 | async-start | bytes 3145728 | tf_op jit(solution)/shard_map/all_to_all | solution.py:593
  557.9 7.6 %concatenate.48 = bf16[768,786]{0,1:T(8,128)(2,1)} concatenate(bf16[768,576]{0,1:T(8,128)(2,1)} %fusion.87, bf16[768,192]{0,1:T(8,128)(2,1)S(1)} %copy-done.18, bf16[768,16]{0,1:T(8,128)(2,1)S(1)} %copy-done.27, bf16[768,1]{0,1:T(2,128)(2,1)S(1)} %broadcast_in_dim.54, bf16[768,1]{0,1:T(2,128)(2,1)S(1)} %broadcast_in_dim.55), dimensions={1} | concatenate | bytes 2414592 | tf_op jit(solution)/shard_map/concatenate | solution.py:604
  570.9 5.4 all-to-all-start.11
  580.7 13.6 %all-to-all-done.11 = bf16[8,96,786]{2,1,0:T(8,128)(2,1)} async-done(((bf16[8,96,786]{2,1,0:T(8,128)(2,1)}), bf16[8,96,786]{2,1,0:T(8,128)(2,1)}, u32[]{:S(2)}, u32[]{:S(2)}) %all-to-all-start.11) | async-done | bytes 1207328 | tf_op jit(solution)/shard_map/all_to_all | solution.py:317
  595.9 6.8 copy.127
  607.6 41.0 %all-reduce.7.cloned.1.call-done = bf16[1024,768]{1,0:T(8,128)(2,1)} async-done(((bf16[1024,768]{1,0:T(8,128)(2,1)}), bf16[1024,768]{1,0:T(8,128)(2,1)}) %all-reduce.7.cloned.1.call-update) | async-done | bytes 1572880 | tf_op jit(solution)/shard_map/psum | solution.py:577
  658.8 19.6 %psum.31 = f32[96,18]{1,0:T(8,128)S(1)} all-reduce(f32[96,18]{1,0:T(8,128)S(1)} %slice.168), channel_id=1, replica_groups=mesh['dp'=2,'ctx'=4,'tensor'=4] {'tensor'}, use_global_device_ids=true, to_apply=%region_14.15 | all-reduce | flops 1728 | bytes 13824 | tf_op jit(solution)/shard_map/psum | solution.py:607
  682.8 37.7 %all-reduce.9.cloned.1.call-done = bf16[1024,768]{1,0:T(8,128)(2,1)} async-done(((bf16[1024,768]{1,0:T(8,128)(2,1)}), bf16[1024,768]{1,0:T(8,128)(2,1)}) %all-reduce.9.cloned.1.call-update) | async-done | bytes 1572880 | tf_op jit(solution)/shard_map/psum | solution.py:599
  729.1 5.5 convert_element_type.194
  (250 shorter events, 208.8 us)
Async XLA Ops:
  7.2 48.6 %all-gather.7.cloned.1.call-start = ((), (), s32[]{:S(2)}) async-start(), calls=%async_computation.13 | async-start | bytes 1548288 | tf_op jit(solution)/shard_map/all_gather | solution.py:368
  12.4 40.7 %all-to-all-start = ((bf16[8,192,512]{2,1,0:T(8,128)(2,1)}), bf16[8,192,512]{2,1,0:T(8,128)(2,1)}, u32[]{:S(2)}, u32[]{:S(2)}) async-start(bf16[8,192,512]{2,1,0:T(8,128)(2,1)} %param.26), calls=%async_computation | async-start | bytes 3145728 | tf_op jit(solution)/shard_map/all_to_all | solution.py:440
  25.4 26.1 %copy-start.1 = (bf16[1,1024,768]{2,1,0:T(8,128)(2,1)S(1)}, bf16[1,1024,768]{2,1,0:T(8,128)(2,1)}, u32[]{:S(2)}) copy-start(bf16[1,1024,768]{2,1,0:T(8,128)(2,1)} %param.14) | copy-start | bytes 4718596
  26.5 44.3 %copy-start.30 = (s32[1024]{0:T(1024)}, s32[1024]{0:T(1024)S(1)}, u32[]{:S(2)}) copy-start(s32[1024]{0:T(1024)S(1)} %get-tuple-element.203) | copy-start | bytes 12292
  26.5 44.3 %copy-start.33 = (s32[1024]{0:T(1024)}, s32[1024]{0:T(1024)S(1)}, u32[]{:S(2)}) copy-start(s32[1024]{0:T(1024)S(1)} %get-tuple-element.204) | copy-start | bytes 12292
  51.4 15.5 %copy-start.38 = (s32[1280]{0:T(1024)}, s32[1280]{0:T(1024)S(1)}, u32[]{:S(2)}) copy-start(s32[1280]{0:T(1024)S(1)} %add.281) | copy-start | bytes 15364
  61.7 13.9 %collective-permute-start.1 = (bf16[384,1024]{1,0:T(8,128)(2,1)S(1)}, bf16[384,1024]{1,0:T(8,128)(2,1)S(1)}, u32[]{:S(2)}, u32[]{:S(2)}) collective-permute-start(bf16[384,1024]{1,0:T(8,128)(2,1)S(1)} %pad_maximum_fusion.6), channel_id=1, source_target_pairs={{0,4},{4,8},{8,12},{1,5},{5,9},{9,13},{2,6},{6,10},{10,14},{3,7},{... | collective-permute-start | bytes 2359304 | tf_op jit(solution)/shard_map/ppermute | solution.py:449
  64.0 19.9 %collective-permute-start = (bf16[384,1024]{1,0:T(8,128)(2,1)S(1)}, bf16[384,1024]{1,0:T(8,128)(2,1)}, u32[]{:S(2)}, u32[]{:S(2)}) collective-permute-start(bf16[384,1024]{1,0:T(8,128)(2,1)S(1)} %pad_maximum_fusion.6), channel_id=1, source_target_pairs={{0,8},{4,12},{1,9},{5,13},{2,10},{6,14},{3,11},{7,15},{16,24},{20,... | collective-permute-start | bytes 2359304 | tf_op jit(solution)/shard_map/ppermute | solution.py:449
  85.5 56.0 %all-to-all-start.1 = ((bf16[8,2,160,768]{3,2,1,0:T(8,128)(2,1)}), bf16[8,2,160,768]{3,2,1,0:T(8,128)(2,1)}, u32[]{:S(2)}, u32[]{:S(2)}) async-start(bf16[8,2,160,768]{3,2,1,0:T(8,128)(2,1)} %pad_maximum_fusion), calls=%async_computation.1 | async-start | bytes 7864320 | tf_op jit(solution)/shard_map/all_to_all | solution.py:384
  95.8 55.4 %all-gather.11.cloned.1.call-start = ((), (), s32[]{:S(2)}) async-start(), calls=%async_computation.18 | async-start | bytes 1966080 | tf_op jit(solution)/shard_map/all_gather | solution.py:371
  141.5 49.1 %all-to-all-start.2 = ((bf16[8,2,192,512]{3,2,1,0:T(8,128)(2,1)}), bf16[8,2,192,512]{3,2,1,0:T(8,128)(2,1)}, u32[]{:S(2)}, u32[]{:S(2)}) async-start(bf16[8,2,192,512]{3,2,1,0:T(8,128)(2,1)} %param.25), calls=%async_computation.2 | async-start | bytes 6291456 | tf_op jit(solution)/shard_map/all_to_all | solution.py:471
  146.3 13.5 %collective-permute-start.4 = (bf16[192,1024]{1,0:T(8,128)(2,1)S(1)}, bf16[192,1024]{1,0:T(8,128)(2,1)S(1)}, u32[]{:S(2)}, u32[]{:S(2)}) collective-permute-start(bf16[192,1024]{1,0:T(8,128)(2,1)S(1)} %copy-done.12), channel_id=1, source_target_pairs={{0,3},{1,0},{2,1},{3,2},{4,7},{5,4},{6,5},{7,6},{8,11},{9,8},{10,9... | collective-permute-start | bytes 1179656 | tf_op jit(solution)/shard_map/ppermute | solution.py:479
  150.2 34.1 %collective-permute-start.3 = (bf16[192,1024]{1,0:T(8,128)(2,1)S(1)}, bf16[192,1024]{1,0:T(8,128)(2,1)S(1)}, u32[]{:S(2)}, u32[]{:S(2)}) collective-permute-start(bf16[192,1024]{1,0:T(8,128)(2,1)S(1)} %copy-done.12), channel_id=1, source_target_pairs={{0,2},{1,3},{2,0},{3,1},{4,6},{5,7},{6,4},{7,5},{8,10},{9,11},{10,... | collective-permute-start | bytes 1179656 | tf_op jit(solution)/shard_map/ppermute | solution.py:479
  150.2 34.1 %collective-permute-start.2 = (bf16[192,1024]{1,0:T(8,128)(2,1)S(1)}, bf16[192,1024]{1,0:T(8,128)(2,1)S(1)}, u32[]{:S(2)}, u32[]{:S(2)}) collective-permute-start(bf16[192,1024]{1,0:T(8,128)(2,1)S(1)} %copy-done.12), channel_id=1, source_target_pairs={{0,1},{1,2},{2,3},{3,0},{4,5},{5,6},{6,7},{7,4},{8,9},{9,10},{10,1... | collective-permute-start | bytes 1179656 | tf_op jit(solution)/shard_map/ppermute | solution.py:479
  159.8 24.5 %copy-start.45 = (bf16[192,1024]{1,0:T(8,128)(2,1)}, bf16[192,1024]{1,0:T(8,128)(2,1)S(1)}, u32[]{:S(2)}) copy-start(bf16[192,1024]{1,0:T(8,128)(2,1)S(1)} %collective-permute-done.4) | copy-start | bytes 1179652
  198.3 28.8 %all-to-all-start.3 = ((bf16[8,1,160,768]{3,2,1,0:T(8,128)(2,1)}), bf16[8,1,160,768]{3,2,1,0:T(8,128)(2,1)}, u32[]{:S(2)}, u32[]{:S(2)}) async-start(bf16[8,1,160,768]{3,2,1,0:T(8,128)(2,1)} %bitcast.125), calls=%async_computation.3 | async-start | bytes 3932160 | tf_op jit(solution)/shard_map/all_to_all | solution.py:384
  208.0 24.0 %copy-start.26 = (bf16[2,96,512]{2,1,0:T(8,128)(2,1)S(1)}, bf16[2,96,512]{2,1,0:T(8,128)(2,1)}, u32[]{:S(2)}) copy-start(bf16[2,96,512]{2,1,0:T(8,128)(2,1)} %param.23) | copy-start | bytes 589828
  227.1 31.9 %all-to-all-start.4 = ((bf16[8,1,160,768]{3,2,1,0:T(8,128)(2,1)}), bf16[8,1,160,768]{3,2,1,0:T(8,128)(2,1)}, u32[]{:S(2)}, u32[]{:S(2)}) async-start(bf16[8,1,160,768]{3,2,1,0:T(8,128)(2,1)} %bitcast.123), calls=%async_computation.4 | async-start | bytes 3932160 | tf_op jit(solution)/shard_map/all_to_all | solution.py:384
  231.6 67.1 %all-gather.9.cloned.1.call-start = ((), (), s32[]{:S(2)}) async-start(), calls=%async_computation.14 | async-start | bytes 2654208 | tf_op jit(solution)/shard_map/all_gather | solution.py:507
  259.1 29.7 %all-to-all-start.5 = ((bf16[8,1,160,768]{3,2,1,0:T(8,128)(2,1)}), bf16[8,1,160,768]{3,2,1,0:T(8,128)(2,1)}, u32[]{:S(2)}, u32[]{:S(2)}) async-start(bf16[8,1,160,768]{3,2,1,0:T(8,128)(2,1)} %get-tuple-element.95), calls=%async_computation.5 | async-start | bytes 3932160 | tf_op jit(solution)/shard_map/all_to_all | solution.py:384
  288.8 28.9 %all-to-all-start.6 = ((bf16[8,1,160,768]{3,2,1,0:T(8,128)(2,1)}), bf16[8,1,160,768]{3,2,1,0:T(8,128)(2,1)}, u32[]{:S(2)}, u32[]{:S(2)}) async-start(bf16[8,1,160,768]{3,2,1,0:T(8,128)(2,1)} %get-tuple-element.96), calls=%async_computation.6 | async-start | bytes 3932160 | tf_op jit(solution)/shard_map/all_to_all | solution.py:384
  353.4 28.6 %all-to-all-start.8 = ((bf16[8,1,160,768]{3,2,1,0:T(8,128)(2,1)}), bf16[8,1,160,768]{3,2,1,0:T(8,128)(2,1)}, u32[]{:S(2)}, u32[]{:S(2)}) async-start(bf16[8,1,160,768]{3,2,1,0:T(8,128)(2,1)} %get-tuple-element.106), calls=%async_computation.8 | async-start | bytes 3932160 | tf_op jit(solution)/shard_map/all_to_all | solution.py:384
  357.8 72.9 %all-reduce.5.cloned.1.call-start = ((), (), s32[]{:S(2)}) async-start(), calls=%async_computation.15 | async-start | bytes 3145728 | tf_op jit(solution)/shard_map/psum | solution.py:563
  465.5 63.9 %all-to-all-start.9 = ((bf16[3,8,96,512]{3,2,0,1:T(8,128)(2,1)}), bf16[3,8,96,512]{3,2,0,1:T(8,128)(2,1)}, u32[]{:S(2)}, u32[]{:S(2)}) async-start(bf16[3,8,96,512]{3,2,0,1:T(8,128)(2,1)} %copy.122), calls=%async_computation.9 | async-start | bytes 4718592 | tf_op jit(solution)/shard_map/all_to_all | solution.py:317
  485.7 39.2 %collective-permute-start.6 = (bf16[384,1024]{1,0:T(8,128)(2,1)S(1)}, bf16[384,1024]{1,0:T(8,128)(2,1)S(1)}, u32[]{:S(2)}, u32[]{:S(2)}) collective-permute-start(bf16[384,1024]{1,0:T(8,128)(2,1)S(1)} %get-tuple-element.212), channel_id=1, source_target_pairs={{8,0},{12,4},{9,1},{13,5},{10,2},{14,6},{11,3},{15,7},{24,16},{28,... | collective-permute-start | bytes 2359304 | tf_op jit(solution)/shard_map/ppermute | solution.py:587
  487.2 37.8 %collective-permute-start.5 = (bf16[384,1024]{1,0:T(8,128)(2,1)S(1)}, bf16[384,1024]{1,0:T(8,128)(2,1)S(1)}, u32[]{:S(2)}, u32[]{:S(2)}) collective-permute-start(bf16[384,1024]{1,0:T(8,128)(2,1)S(1)} %get-tuple-element.211), channel_id=1, source_target_pairs={{4,0},{8,4},{12,8},{5,1},{9,5},{13,9},{6,2},{10,6},{14,10},{7,3},{... | collective-permute-start | bytes 2359304 | tf_op jit(solution)/shard_map/ppermute | solution.py:587
  535.1 30.4 %all-to-all-start.10 = ((bf16[2,768,512]{2,0,1:T(2,128)(2,1)}), bf16[2,768,512]{2,0,1:T(2,128)(2,1)}, u32[]{:S(2)}, u32[]{:S(2)}) async-start(bf16[2,768,512]{2,0,1:T(2,128)(2,1)} %copy.124), calls=%async_computation.10 | async-start | bytes 3145728 | tf_op jit(solution)/shard_map/all_to_all | solution.py:593
  570.9 23.5 %all-to-all-start.11 = ((bf16[8,96,786]{2,1,0:T(8,128)(2,1)}), bf16[8,96,786]{2,1,0:T(8,128)(2,1)}, u32[]{:S(2)}, u32[]{:S(2)}) async-start(bf16[8,96,786]{2,1,0:T(8,128)(2,1)} %bitcast.117), calls=%async_computation.11 | async-start | bytes 2752512 | tf_op jit(solution)/shard_map/all_to_all | solution.py:317
  576.3 72.2 %all-reduce.7.cloned.1.call-start = ((), (), s32[]{:S(2)}) async-start(), calls=%async_computation.16 | async-start | bytes 3145728 | tf_op jit(solution)/shard_map/psum | solution.py:577
  602.7 75.8 %all-to-all-start.12 = ((bf16[2,2,768,512]{3,1,0,2:T(2,128)(2,1)}), bf16[2,2,768,512]{3,1,0,2:T(2,128)(2,1)}, u32[]{:S(2)}, u32[]{:S(2)}) async-start(bf16[2,2,768,512]{3,1,0,2:T(2,128)(2,1)} %copy.127), calls=%async_computation.12 | async-start | bytes 6291456 | tf_op jit(solution)/shard_map/all_to_all | solution.py:611
  607.4 113.2 %all-reduce.9.cloned.1.call-start = ((), (), s32[]{:S(2)}) async-start(), calls=%async_computation.17 | async-start | bytes 3145728 | tf_op jit(solution)/shard_map/psum | solution.py:599
  682.8 40.5 %copy-start = (f32[1024,768]{1,0:T(8,128)S(1)}, f32[1024,768]{1,0:T(8,128)}, u32[]{:S(2)}) copy-start(f32[1024,768]{1,0:T(8,128)} %multiply_add_fusion) | copy-start | bytes 9437188
  (44 other events, 226.5 us)
Sparse Core Ops, SparseCore 0:
  12.5 32.4 all-gather.6
  99.1 39.0 all-gather.10
  234.9 35.1 all-gather.8
  361.2 69.3 all-reduce.4
  579.7 68.7 all-reduce.6
  650.8 69.7 all-reduce.8

commit v2 on v1

--- a/solution.py
+++ b/solution.py
@@ -227,13 +227,15 @@
 
     @pl.when(step == pl.num_programs(1) - 1)
     def _():
-        gin_ref[0] = acc_in[...].astype(BF)
-        gout_ref[0] = acc_out[...].astype(BF)
+        cut = gin_ref.shape[3]
+        for n in range(gin_ref.shape[0]):
+            gin_ref[n, 0] = acc_in[:, n * cut : (n + 1) * cut].astype(BF)
+            gout_ref[n, 0] = acc_out[n * cut : (n + 1) * cut].astype(BF)
         if gated:
             grouter_ref[...] = acc_router[...]
 
 
-def ffn(x, g, w_in, w_out, block, routing=None, at=0):
+def ffn(x, g, w_in, w_out, block, parts, routing=None, at=0):
     sources, experts, rows, width = x.shape
     units = w_out.shape[2]
     gated = routing is not None
@@ -242,18 +244,19 @@
     big_at = pl.BlockSpec((block, 1, rows, width), lambda e, s, *_: (s, at + e, 0, 0))
     w_in_at = pl.BlockSpec((1, 2, width, units), lambda e, s, *_: (at + e, 0, 0, 0))
     w_out_at = pl.BlockSpec((1, width, units), lambda e, s, *_: (at + e, 0, 0))
-    w_in_spec = pl.BlockSpec((1, 2, width, units), lambda e, s, *_: (e, 0, 0, 0))
-    w_out_spec = pl.BlockSpec((1, width, units), lambda e, s, *_: (e, 0, 0))
+    cut = width // parts
+    g_in_spec = pl.BlockSpec((parts, 1, 2, cut, units), lambda e, s, *_: (0, e, 0, 0, 0))
+    g_out_spec = pl.BlockSpec((parts, 1, cut, units), lambda e, s, *_: (0, e, 0, 0))
     wide = jax.ShapeDtypeStruct(x.shape, BF)
     ins = [x, g]
     in_specs = [big, big_at]
     outs = [
         wide,
         wide,
-        jax.ShapeDtypeStruct((experts, 2, width, units), BF),
-        jax.ShapeDtypeStruct((experts, width, units), BF),
+        jax.ShapeDtypeStruct((parts, experts, 2, cut, units), BF),
+        jax.ShapeDtypeStruct((parts, experts, cut, units), BF),
     ]
-    out_specs = [big, big, w_in_spec, w_out_spec]
+    out_specs = [big, big, g_in_spec, g_out_spec]
     scratch = [pltpu.VMEM((2, width, units), F32), pltpu.VMEM((width, units), F32)]
     if gated:
         first, other, router = routing
@@ -355,23 +358,23 @@
     heads_cols = qkv_weight.shape[2]
     qkv_cols = 3 * heads_cols
     experts = router_weight.shape[1]
-    thin = jnp.concatenate(
-        [
-            qkv_weight.transpose(1, 0, 2).reshape(-1, qkv_cols),
-            out_weight,
-            router_weight,
-            gain_attn[:, None],
-            gain_ffn[:, None],
-        ],
+    tensor_count = lax.axis_size("tensor")
+    first_w = jnp.concatenate(
+        [qkv_weight.transpose(1, 0, 2).reshape(-1, qkv_cols), gain_attn[:, None]], axis=1
+    )
+    first_full = lax.all_gather(first_w, DC, axis=0, tiled=True)
+    qkv_full = first_full[:, :qkv_cols]
+    attn_gain = first_full[:, qkv_cols].astype(F32)
+    rings = [
+        [(i, (i + hop) % tensor_count) for i in range(tensor_count)]
+        for hop in range(1, tensor_count)
+    ]
+    second_w = jnp.concatenate(
+        [out_weight]
+        + [lax.ppermute(out_weight, "tensor", links) for links in rings]
+        + [router_weight, gain_ffn[:, None]],
         axis=1,
     )
-    thin_full = lax.all_gather(thin, DC, axis=0, tiled=True)
-    qkv_full = thin_full[:, :qkv_cols]
-    out_full = thin_full[:, qkv_cols : qkv_cols + heads_cols]
-    out_tensor = lax.all_gather(out_full, "tensor", axis=0)
-    router_full = thin_full[:, qkv_cols + heads_cols : qkv_cols + heads_cols + experts]
-    attn_gain = thin_full[:, -2].astype(F32)
-    ffn_gain = thin_full[:, -1].astype(F32)
 
     local_experts = expert_in.shape[0]
     spread = local_experts % ctx_count == 0
@@ -391,25 +394,8 @@
         ).reshape(-1)
         for n in range(own)
     ]
-    owner_at = lax.axis_index(expert_axes)
-    first = owner_at * own
+    first = lax.axis_index(expert_axes) * own
     my_slots = first * capacity + jnp.arange(own * capacity, dtype=jnp.int32)
-    pairs = lax.all_gather(
-        jnp.stack([place[:, 0], place[:, 1], my_routes[:, 1], my_routes[:, 0]]),
-        expert_axes,
-        axis=0,
-    )
-    slot_other = (
-        jnp.sum(
-            jnp.where(
-                pairs[:, :2, None, :] == my_slots[None, None, :, None],
-                pairs[:, 2:, None, :] + 1,
-                0,
-            ),
-            axis=(1, 3),
-        )
-        - 1
-    ).reshape(owners, own, capacity, 1)
     to_slot = [
         ((place[None, :, 0] == ids[:, None]) | (place[None, :, 1] == ids[:, None])).astype(BF)
         for ids in block_ids
@@ -432,15 +418,16 @@
     inverse = 1.0 / 10000.0 ** (jnp.arange(HALF, dtype=F32) * (2.0 / HD))
     angles = inverse[:, None] * query_pos.astype(F32)[None, :]
     cos_t, sin_t = jnp.cos(angles), jnp.sin(angles)
+    expert_out, qkv_full = tie(expert_out, qkv_full)
+    if spread:
+        eout = lax.all_to_all(expert_out, "ctx", split_axis=0, concat_axis=1, tiled=True)
+    else:
+        eout = lax.all_gather(expert_out, "ctx", axis=1, tiled=True)
     raw_t = jnp.einsum("dc,ld->cl", qkv_full, normed, preferred_element_type=F32)
     q_t = half_turn(raw_t[:heads_cols], cos_t, sin_t).astype(BF)
     k_t = half_turn(raw_t[heads_cols : 2 * heads_cols], cos_t, sin_t).astype(BF)
     v_t = raw_t[2 * heads_cols :].astype(BF)
-    if spread:
-        eout = lax.all_to_all(expert_out, "ctx", split_axis=0, concat_axis=1, tiled=True)
-    else:
-        eout = lax.all_gather(expert_out, "ctx", axis=1, tiled=True)
-    kv_t, slot_other, eout = tie(jnp.concatenate([k_t, v_t], axis=0), slot_other, eout)
+    kv_t = jnp.concatenate([k_t, v_t], axis=0)
     before = min(ctx_count - 1, -(-(LONGEST - 1) // rows))
     shift = before * rows
     pieces = [kv_t]
@@ -448,10 +435,15 @@
         links = [(i, i + hop) for i in range(ctx_count - hop)]
         pieces.insert(0, lax.ppermute(kv_t, "ctx", links))
     kv_win = jnp.concatenate(pieces, axis=1)
-    kv_win, slot_g = tie(kv_win, slot_g)
+    kv_win, slot_g, second_w, eout = tie(kv_win, slot_g, second_w, eout)
     k_win, v_win = kv_win[:heads_cols], kv_win[heads_cols:]
 
     got_g = swap(slot_g)
+    second_full = lax.all_gather(second_w, DC, axis=0, tiled=True)
+    out_all = second_full[:, : tensor_count * heads_cols]
+    out_full = out_all[:, :heads_cols]
+    router_full = second_full[:, tensor_count * heads_cols : -1]
+    ffn_gain = second_full[:, -1].astype(F32)
 
     starts = jnp.sum(
         seg_all[:, None] < jnp.arange(DOCS, dtype=jnp.int32)[None, :], axis=0, dtype=jnp.int32
@@ -466,27 +458,31 @@
     lo = jnp.maximum(doc[::BQ], 0) // BK
     doc = doc[None, :]
     att_t, lse = attn_forward(lo, q_t, k_win, v_win, doc, shift)
-    expert_in, lse, got_g = tie(expert_in, lse, got_g)
+    place, expert_in, lse, got_g = tie(place, expert_in, lse, got_g)
     if spread:
         ein = lax.all_to_all(expert_in, "ctx", split_axis=0, concat_axis=2, tiled=True)
     else:
         ein = lax.all_gather(expert_in, "ctx", axis=2, tiled=True)
-    tensor_count = lax.axis_size("tensor")
-    tensor_at = lax.axis_index("tensor")
-    att_parts, out_parts = [att_t], [out_full]
-    for hop in range(1, tensor_count):
-        links = [(i, (i + hop) % tensor_count) for i in range(tensor_count)]
-        att_parts.append(lax.ppermute(att_t, "tensor", links))
-        out_parts.append(
-            lax.dynamic_index_in_dim(
-                out_tensor, (tensor_at - hop) % tensor_count, 0, keepdims=False
-            )
+    pairs = lax.all_gather(
+        jnp.stack([place[:, 0], place[:, 1], my_routes[:, 1], my_routes[:, 0]]),
+        expert_axes,
+        axis=0,
+    )
+    slot_other = (
+        jnp.sum(
+            jnp.where(
+                pairs[:, :2, None, :] == my_slots[None, None, :, None],
+                pairs[:, 2:, None, :] + 1,
+                0,
+            ),
+            axis=(1, 3),
         )
+        - 1
+    ).reshape(owners, own, capacity, 1)
+    att_parts = [att_t] + [lax.ppermute(att_t, "tensor", links) for links in rings]
+    att_parts[-1], slot_other = tie(att_parts[-1], slot_other)
     branch = jnp.einsum(
-        "cl,dc->ld",
-        jnp.concatenate(att_parts, axis=0),
-        jnp.concatenate(out_parts, axis=1),
-        preferred_element_type=F32,
+        "cl,dc->ld", jnp.concatenate(att_parts, axis=0), out_all, preferred_element_type=F32
     )
     branch = with_layout_constraint(branch, Layout((0, 1)))
     resid = inputs + branch
@@ -514,6 +510,7 @@
             ein,
             eout,
             4,
+            ctx_count,
             (jnp.reshape(first + n, (1,)).astype(jnp.int32), slot_other, router_wide),
             n,
         )
@@ -527,8 +524,14 @@
             dx, back_dx[-1] = tie(dx, back_dx[-1])
         back_dx.append(swap(dx).reshape(-1, width))
     router_part = sum(routers)[:, :experts]
-    g_ein = jnp.concatenate(g_eins, axis=0)
-    g_eout = jnp.concatenate(g_eouts, axis=0)
+    g_ein = jnp.concatenate(g_eins, axis=1)
+    g_eout = jnp.concatenate(g_eouts, axis=1)
+
+    def to_owner(values):
+        if spread:
+            swapped = lax.all_to_all(values, "ctx", split_axis=0, concat_axis=0, tiled=True)
+            return swapped.reshape((-1,) + values.shape[2:])
+        return lax.psum_scatter(values, "ctx", scatter_dimension=0, tiled=True)[0]
 
     parts = 4
     shared_shape = (parts, 1, rows // parts, width)
@@ -538,6 +541,7 @@
         shared_full[None, :2],
         shared_full[None, 2],
         2,
+        lax.axis_size(DC),
     )
     back_dx[-1], sh_dx = lax.optimization_barrier((back_dx[-1], sh_dx))
 
@@ -554,16 +558,18 @@
 
     dn2_part = at_tokens(back_dx, sh_dx)
     dn2_low = dn2_part.astype(BF)
-    ys[0], dn2_low = tie(ys[0], dn2_low)
+    dn2 = lax.psum(dn2_low, "tensor")
+    sh_grad, dn2_low = tie(jnp.concatenate([sh_gin[:, 0], sh_gout], axis=1), dn2_low)
+    shared_parts = lax.all_to_all(sh_grad, DC, split_axis=0, concat_axis=0, tiled=True)
+    ys[0], shared_parts = tie(ys[0], shared_parts)
+    total_shared = jnp.sum(shared_parts.astype(F32), axis=0)
     back_y = []
     for y in ys:
         if back_y:
             y, back_y[-1] = tie(y, back_y[-1])
         back_y.append(swap(y).reshape(-1, width))
-    dn2 = lax.psum(dn2_low, "tensor")
-    sh_grad, back_y[-1] = tie(jnp.concatenate([sh_gin[0], sh_gout], axis=0), back_y[-1])
-    total_shared = own_sum(sh_grad, 1)
-    dn2, back_y[-1] = tie(dn2, back_y[-1])
+    g_eout, back_y[-1] = tie(g_eout, back_y[-1])
+    grad_eout = to_owner(g_eout)
     dn2 = dn2.astype(F32)
     gain2_part = jnp.sum(dn2_part * n2, axis=0)
 
@@ -588,30 +594,28 @@
     dq_raw = half_turn(dq_t, cos_t, -sin_t)
     dk_raw = half_turn(dkv[:heads_cols], cos_t, -sin_t)
     draw_t = jnp.concatenate([dq_raw, dk_raw, dkv[heads_cols:]], axis=0).astype(BF)
-    g_eout, draw_t, total_shared = tie(g_eout, draw_t, total_shared)
-    if spread:
-        grad_eout = lax.all_to_all(g_eout, "ctx", split_axis=1, concat_axis=0, tiled=True)
-    else:
-        grad_eout = lax.psum_scatter(g_eout, "ctx", scatter_dimension=1, tiled=True)
+    g_ein, draw_t, grad_eout = tie(g_ein, draw_t, grad_eout)
+    grad_ein = to_owner(g_ein)
     dn1_part = jnp.einsum("cl,dc->ld", draw_t, qkv_full, preferred_element_type=F32)
     dn1_low, ffn_total = lax.optimization_barrier((dn1_part.astype(BF), ffn_total))
     layer_out = (resid + ffn_total.astype(F32)).astype(BF)
     dn1 = lax.psum(dn1_low, "tensor")
     gain1_part = jnp.sum(dn1_part * n1, axis=0)
-    grad_qkv = jnp.einsum("ld,cl->dc", normed, draw_t, preferred_element_type=F32)
-    grad_outw = jnp.einsum("ld,cl->dc", dbranch, att_t, preferred_element_type=F32)
-    small = jnp.concatenate([router_part, gain1_part[:, None], gain2_part[:, None]], axis=1)
-    mixed, grad_eout = tie(jnp.concatenate([grad_qkv, grad_outw, small], axis=1), grad_eout)
+    grad_qkv = with_layout_constraint(
+        jnp.einsum("ld,cl->dc", normed, draw_t, preferred_element_type=F32).astype(BF),
+        Layout((0, 1)),
+    )
+    grad_outw = with_layout_constraint(
+        jnp.einsum("ld,cl->dc", dbranch, att_t, preferred_element_type=F32).astype(BF),
+        Layout((0, 1)),
+    )
+    small = jnp.concatenate([router_part, gain1_part[:, None], gain2_part[:, None]], axis=1).astype(BF)
+    mixed, grad_ein = tie(jnp.concatenate([grad_qkv, grad_outw, small], axis=1), grad_ein)
     tail = own_sum(mixed, 0)
-    g_ein, tail = tie(g_ein, tail)
     small = lax.psum(tail[:, 4 * heads_cols :], "tensor")
     total_qkv = tail[:, : 3 * heads_cols].reshape(-1, 3, heads_cols).transpose(1, 0, 2)
     total_outw = tail[:, 3 * heads_cols : 4 * heads_cols]
-    if spread:
-        grad_ein = lax.all_to_all(g_ein, "ctx", split_axis=2, concat_axis=0, tiled=True)
-    else:
-        grad_ein = lax.psum_scatter(g_ein, "ctx", scatter_dimension=2, tiled=True)
-    dn1, small, grad_ein = tie(dn1, small, grad_ein)
+    dn1, small = tie(dn1, small)
     dn1 = dn1.astype(F32)
     scaled1 = attn_gain * dn1
     grad_tokens = dresid + inv1 * (

time: 751 us -> 704 us (0.937)
  waiting for transfers between devices: 295 us -> 245 us
  blocking collectives: 70.8 us -> 105 us
  local copies, waits for them, and re-layouts: 75.6 us -> 42.9 us
  matrix products: 63.5 us -> 74.6 us
    ppermute x3 -> x6, waiting for transfers between devices: 31.8 us -> 0.02 us  [the longest x3 0.01 us: shards(): lax.ppermute(out_weight, 'tensor', links)]
    all_gather x2 -> x1, waiting for transfers between devices: 0.01 us -> 27.4 us  [shards(): second_full = lax.all_gather(second_w, DC, axis=0, tiled=True)]
    all_to_all x6 -> x7, waiting for transfers between devices: 79.2 us -> 55.1 us  [swap(): lax.all_to_all(values, expert_axes, split_axis=0, concat_axis=0, tiled=True)]
    psum x1, waiting for transfers between devices: 41 us -> 62.2 us  [shards(): ffn_total = lax.psum(ffn_low, 'tensor')]
    all_gather x1, blocking collectives: 21.7 us -> 40.7 us  [shards(): lax.all_gather(jnp.stack([place[:, 0], place[:, 1], my_routes[:, 1], my_r...]
    psum x1, waiting for transfers between devices: 37.7 us -> 19.2 us  [shards(): dn1 = lax.psum(dn1_low, 'tensor')]
    all_to_all x2 -> x1, starting transfers between devices: 19.5 us -> 4.28 us  [own_sum(): lax.all_to_all(parts.astype(BF).reshape(cut), DC, split_axis=axis, concat...]
    all_gather x0 -> x1, blocking collectives: none -> 12.3 us  [shards(): first_full = lax.all_gather(first_w, DC, axis=0, tiled=True)]
  transfers between devices with their start and end apart: 25 -> 27, of which waited for: 14 -> 12; matrix products, arithmetic and copies ran while one was open for 17% -> 18% of each run, Pallas kernels for 8% -> 8%
where the time goes in v2:
time: 704 us; the launch traced here: 698 us
  waiting for transfers between devices  245 us (35%)
  blocking collectives  105 us (15%)
  starting transfers between devices  83 us (12%)
  matrix products  74.6 us (11%)
  Pallas kernels  71.5 us (10%)
  other arithmetic  60.5 us (9%)
  local copies, waits for them, and re-layouts  42.9 us (6%)
  between operations  15 us (2%)
    psum x1, waiting for transfers between devices, shards(): ffn_total = lax.psum(ffn_low, 'tensor')  62.2 us
    all_to_all x7, waiting for transfers between devices, swap(): lax.all_to_all(values, expert_axes, split_axis=0, concat_axis=0, tiled=True)  55.1 us
    pallas_call x3, Pallas kernels, ffn(): pl.pallas_call(functools.partial(ffn_kernel, gated=gated), out_shape=outs...  49.6 us
    psum x1, waiting for transfers between devices, shards(): dn2 = lax.psum(dn2_low, 'tensor')  44.1 us
    all_gather x1, blocking collectives, shards(): lax.all_gather(jnp.stack([place[:, 0], place[:, 1], my_routes[:, 1], my_r...  40.7 us
    all_to_all x1, blocking collectives, shards(): lax.all_to_all(sh_grad, DC, split_axis=0, concat_axis=0, tiled=True)  33.2 us
    all_to_all x7, starting transfers between devices, swap(): lax.all_to_all(values, expert_axes, split_axis=0, concat_axis=0, tiled=True)  31.8 us
    all_gather x1, waiting for transfers between devices, shards(): second_full = lax.all_gather(second_w, DC, axis=0, tiled=True)  27.4 us
  transfers between devices with their start and end apart: 27, of which 12 were waited for; matrix products, arithmetic and copies ran while one was open for 18% of the time, Pallas kernels for 8%

profile of v2, /device:TPU:0, one launch (start us, length us, event | category | flops | bytes accessed | tf_op | source)
XLA Modules:
  0.0 697.6 jit_solution(10977061041212637019)
XLA Ops:
  9.2 12.3 %all_gather.15 = bf16[768,577]{1,0:T(8,128)(2,1)S(1)} all-gather(bf16[96,577]{1,0:T(8,128)(2,1)S(1)} %copy.88), channel_id=1, replica_groups=mesh['dp'=2,'ctx'=4,'tensor'=4] {'dp','ctx'}, dimensions={0}, use_global_device_ids=true | all-gather | bytes 997056 | tf_op jit(solution)/shard_map/all_gather | solution.py:365
  39.9 4.7 all-to-all-start
  58.0 14.2 %fusion.17 = bf16[1280,768]{1,0:T(8,128)(2,1)S(1)} fusion(s32[1024]{0:T(1024)S(1)} %get-tuple-element.206, s32[1024]{0:T(1024)S(1)} %get-tuple-element.205, s32[1280]{0:T(1024)S(1)} %add.253, bf16[1,1024,768]{2,1,0:T(8,128)(2,1)S(1)} %copy-done.5), kind=kOutput, calls=%fused_computation.30 | convolution fusion | flops 2018181120 | bytes 3552256 | tf_op jit(solution)/shard_map/dot_general | solution.py:405
  80.1 4.7 all-to-all-start.1
  91.4 8.5 %attn_fwd.1 = (bf16[192,1024]{1,0:T(8,128)(2,1)}, f32[3,1024]{1,0:T(4,128)}) custom-call(s32[2]{0:T(128)} %and_select_fusion.lo_ref, bf16[192,1024]{1,0:T(8,128)(2,1)} %bitcast.104, bf16[192,3072]{1,0:T(8,128)(2,1)} %get-tuple-element.214.k_ref, bf16[192,3072]{1,0:T(8,128)(2,1)} %get-tuple-element.213.v_ref, s32[1,1024]{1,0:T(1,128)} %bitcast.126), custom_call_target="tpu_custom_call" | custom-call | tf_op jit(solution)/shard_map/attn_fwd/pallas_call | solution.py:132
  102.2 27.4 %all-gather.5.cloned.1.call-done = bf16[768,785]{1,0:T(8,128)(2,1)} async-done(((bf16[96,785]{1,0:T(8,128)(2,1)}), bf16[768,785]{1,0:T(8,128)(2,1)}) %all-gather.5.cloned.1.call-update) | async-done | bytes 1205776 | tf_op jit(solution)/shard_map/all_gather | solution.py:442
  130.8 4.8 all-to-all-done.1.refs_2_
  135.6 4.8 all-to-all-start.2
  141.0 40.7 %all-gather.1 = s32[8,4,1024]{2,1,0:T(4,128)S(1)} all-gather(s32[1,4,1024]{2,1,0:T(4,128)S(1)} %add_bitcast_fusion), channel_id=2, replica_groups=mesh['dp'=2,'ctx'=4,'tensor'=4] {'dp','ctx'}, dimensions={0}, use_global_device_ids=true | all-gather | bytes 147456 | tf_op jit(solution)/shard_map/all_gather | solution.py:466
  203.7 5.2 fusion.18
  209.0 19.1 %all-to-all-done.3.refs_1_ = bf16[8,1,160,768]{3,2,1,0:T(8,128)(2,1)} async-done(((bf16[8,1,160,768]{3,2,1,0:T(8,128)(2,1)}), bf16[8,1,160,768]{3,2,1,0:T(8,128)(2,1)}, u32[]{:S(2)}, u32[]{:S(2)}) %all-to-all-start.3) | async-done | bytes 1966112 | tf_op jit(solution)/shard_map/all_to_all | solution.py:387
  237.4 18.2 %ffn_experts.2 = (bf16[8,1,160,768]{3,2,1,0:T(8,128)(2,1)}, bf16[8,1,160,768]{3,2,1,0:T(8,128)(2,1)}, bf16[4,1,2,192,512]{4,3,2,1,0:T(8,128)(2,1)}, bf16[4,1,192,512]{3,2,1,0:T(8,128)(2,1)}, f32[768,128]{1,0:T(8,128)}) custom-call(s32[1]{0:T(128)} %bitcast.22.refs_0_, bf16[8,1,160,768]{3,2,1,0:T(8,128)(2,1)} %all-to-all-done.3.refs_1_, ...), custom_call_target="tpu_custom_call" | custom-call | tf_op jit(solution)/shard_map/ffn_experts/pallas_call | solution.py:270
  260.0 4.8 all-to-all-start.5
  264.8 18.3 %ffn_experts.3 = (bf16[8,1,160,768]{3,2,1,0:T(8,128)(2,1)}, bf16[8,1,160,768]{3,2,1,0:T(8,128)(2,1)}, bf16[4,1,2,192,512]{4,3,2,1,0:T(8,128)(2,1)}, bf16[4,1,192,512]{3,2,1,0:T(8,128)(2,1)}, f32[768,128]{1,0:T(8,128)}) custom-call(s32[1]{0:T(128)} %bitcast.28.refs_0_, bf16[8,1,160,768]{3,2,1,0:T(8,128)(2,1)} %all-to-all-done.4.refs_1_, ...), custom_call_target="tpu_custom_call" | custom-call | tf_op jit(solution)/shard_map/ffn_experts/pallas_call | solution.py:270
  283.1 6.0 all-to-all-done.5
  293.6 5.4 fusion.14
  303.8 13.1 %ffn_shared.1 = (bf16[4,1,256,768]{3,2,1,0:T(8,128)(2,1)}, bf16[4,1,256,768]{3,2,1,0:T(8,128)(2,1)}, bf16[8,1,2,96,512]{4,3,2,1,0:T(8,128)(2,1)}, bf16[8,1,96,512]{3,2,1,0:T(8,128)(2,1)}) custom-call(bf16[4,1,256,768]{3,2,1,0:T(8,128)(2,1)} %bitcast.102, bf16[4,1,256,768]{3,2,1,0:T(8,128)(2,1)} %bitcast.101, ...), custom_call_target="tpu_custom_call" | custom-call | tf_op jit(solution)/shard_map/ffn_shared/pallas_call | solution.py:270
  320.1 6.4 fusion.88
  326.5 33.2 %all_to_all.91 = bf16[8,3,96,512]{3,2,1,0:T(8,128)(2,1)} all-to-all(bf16[8,3,96,512]{3,2,1,0:T(8,128)(2,1)} %pad_maximum_fusion.2), channel_id=1, replica_groups=mesh['dp'=2,'ctx'=4,'tensor'=4] {'dp','ctx'}, dimensions={0} | all-to-all | bytes 4718592 | tf_op jit(solution)/shard_map/all_to_all | solution.py:563
  367.5 20.9 %all-to-all-done.8 = bf16[8,1,160,768]{3,2,1,0:T(8,128)(2,1)} async-done(((bf16[8,1,160,768]{3,2,1,0:T(8,128)(2,1)}), bf16[8,1,160,768]{3,2,1,0:T(8,128)(2,1)}, u32[]{:S(2)}, u32[]{:S(2)}) %all-to-all-start.8) | async-done | bytes 1966112 | tf_op jit(solution)/shard_map/all_to_all | solution.py:387
  393.0 44.1 %all-reduce.5.cloned.1.call-done = bf16[1024,768]{1,0:T(8,128)(2,1)} async-done(((bf16[1024,768]{1,0:T(8,128)(2,1)}), bf16[1024,768]{1,0:T(8,128)(2,1)}) %all-reduce.5.cloned.1.call-update) | async-done | bytes 1572880 | tf_op jit(solution)/shard_map/psum | solution.py:561
  445.0 5.4 fusion.13
  450.4 5.9 fusion.31
  456.3 13.4 %attn_bwd.1 = (f32[192,1024]{1,0:T(8,128)}, f32[192,3072]{1,0:T(8,128)}, f32[192,3072]{1,0:T(8,128)}) custom-call(s32[2]{0:T(128)} %and_select_fusion.lo_ref, bf16[192,1024]{1,0:T(8,128)(2,1)} %bitcast.105, bf16[192,3072]{1,0:T(8,128)(2,1)} %get-tuple-element.214.k_ref, bf16[192,3072]{1,0:T(8,128)(2,1)} %get-tuple-element.213.v_ref, ...), custom_call_target="tpu_custom_call" | custom-call | tf_op jit(solution)/shard_map/attn_bwd/pallas_call | solution.py:152
  478.3 14.3 %all-to-all-start.10 = ((bf16[4,2,192,512]{3,2,1,0:T(8,128)(2,1)}), bf16[4,2,192,512]{3,2,1,0:T(8,128)(2,1)}, u32[]{:S(2)}, u32[]{:S(2)}) async-start(bf16[4,2,192,512]{3,2,1,0:T(8,128)(2,1)} %pad_maximum_fusion.3), calls=%async_computation.10 | async-start | bytes 3145728 | tf_op jit(solution)/shard_map/all_to_all | solution.py:532
  496.5 26.5 %collective-permute-done.9 = bf16[384,1024]{1,0:T(8,128)(2,1)} collective-permute-done((bf16[384,1024]{1,0:T(8,128)(2,1)}, bf16[384,1024]{1,0:T(8,128)(2,1)}, u32[]{:S(2)}, u32[]{:S(2)}) %collective-permute-start.9) | collective-permute-done | bytes 786464 | tf_op jit(solution)/shard_map/ppermute | solution.py:593
  527.8 5.0 all-to-all-done.10
  532.8 4.7 all-to-all-start.11
  548.2 62.2 %all-reduce.7.cloned.1.call-done = bf16[1024,768]{1,0:T(8,128)(2,1)} async-done(((bf16[1024,768]{1,0:T(8,128)(2,1)}), bf16[1024,768]{1,0:T(8,128)(2,1)}) %all-reduce.7.cloned.1.call-update) | async-done | bytes 1572880 | tf_op jit(solution)/shard_map/psum | solution.py:583
  631.8 5.5 convert_element_type.199
  643.3 18.7 %psum.31 = f32[96,18]{1,0:T(8,128)S(1)} all-reduce(f32[96,18]{1,0:T(8,128)S(1)} %slice.220), channel_id=1, replica_groups=mesh['dp'=2,'ctx'=4,'tensor'=4] {'tensor'}, use_global_device_ids=true, to_apply=%region_13.14 | all-reduce | flops 1728 | bytes 13824 | tf_op jit(solution)/shard_map/psum | solution.py:615
  662.0 19.2 %all-reduce.9.cloned.1.call-done = bf16[1024,768]{1,0:T(8,128)(2,1)} async-done(((bf16[1024,768]{1,0:T(8,128)(2,1)}), bf16[1024,768]{1,0:T(8,128)(2,1)}) %all-reduce.9.cloned.1.call-update) | async-done | bytes 1572880 | tf_op jit(solution)/shard_map/psum | solution.py:602
  (253 shorter events, 185.1 us)
Async XLA Ops:
  27.1 48.5 %collective-permute-start = (bf16[384,1024]{1,0:T(8,128)(2,1)}, bf16[384,1024]{1,0:T(8,128)(2,1)}, u32[]{:S(2)}, u32[]{:S(2)}) collective-permute-start(bf16[384,1024]{1,0:T(8,128)(2,1)} %pad_maximum_fusion.5), channel_id=1, source_target_pairs={{0,8},{4,12},{1,9},{5,13},{2,10},{6,14},{3,11},{7,15},{16,24},{20,... | collective-permute-start | bytes 2359304 | tf_op jit(solution)/shard_map/ppermute | solution.py:436
  31.5 44.1 %collective-permute-start.1 = (bf16[384,1024]{1,0:T(8,128)(2,1)}, bf16[384,1024]{1,0:T(8,128)(2,1)}, u32[]{:S(2)}, u32[]{:S(2)}) collective-permute-start(bf16[384,1024]{1,0:T(8,128)(2,1)} %pad_maximum_fusion.5), channel_id=1, source_target_pairs={{0,4},{4,8},{8,12},{1,5},{5,9},{9,13},{2,6},{6,10},{10,14},{3,7},{... | collective-permute-start | bytes 2359304 | tf_op jit(solution)/shard_map/ppermute | solution.py:436
  34.4 40.4 %collective-permute-start.2 = (bf16[96,192]{1,0:T(8,128)(2,1)S(1)}, bf16[96,192]{1,0:T(8,128)(2,1)S(1)}, u32[]{:S(2)}, u32[]{:S(2)}) collective-permute-start(bf16[96,192]{1,0:T(8,128)(2,1)S(1)} %copy-done.26), channel_id=1, source_target_pairs={{0,1},{1,2},{2,3},{3,0},{4,5},{5,6},{6,7},{7,4},{8,9},{9,10},{10,1... | collective-permute-start | bytes 110600 | tf_op jit(solution)/shard_map/ppermute | solution.py:374
  36.0 38.8 %collective-permute-start.3 = (bf16[96,192]{1,0:T(8,128)(2,1)S(1)}, bf16[96,192]{1,0:T(8,128)(2,1)S(1)}, u32[]{:S(2)}, u32[]{:S(2)}) collective-permute-start(bf16[96,192]{1,0:T(8,128)(2,1)S(1)} %copy-done.26), channel_id=1, source_target_pairs={{0,2},{1,3},{2,0},{3,1},{4,6},{5,7},{6,4},{7,5},{8,10},{9,11},{10,... | collective-permute-start | bytes 110600 | tf_op jit(solution)/shard_map/ppermute | solution.py:374
  38.6 36.2 %collective-permute-start.4 = (bf16[96,192]{1,0:T(8,128)(2,1)S(1)}, bf16[96,192]{1,0:T(8,128)(2,1)S(1)}, u32[]{:S(2)}, u32[]{:S(2)}) collective-permute-start(bf16[96,192]{1,0:T(8,128)(2,1)S(1)} %copy-done.26), channel_id=1, source_target_pairs={{0,3},{1,0},{2,1},{3,2},{4,7},{5,4},{6,5},{7,6},{8,11},{9,8},{10,9... | collective-permute-start | bytes 110600 | tf_op jit(solution)/shard_map/ppermute | solution.py:374
  39.9 37.5 %all-to-all-start = ((bf16[8,192,512]{2,1,0:T(8,128)(2,1)}), bf16[8,192,512]{2,1,0:T(8,128)(2,1)}, u32[]{:S(2)}, u32[]{:S(2)}) async-start(bf16[8,192,512]{2,1,0:T(8,128)(2,1)} %param.26), calls=%async_computation | async-start | bytes 3145728 | tf_op jit(solution)/shard_map/all_to_all | solution.py:423
  80.1 55.5 %all-to-all-start.1 = ((bf16[8,2,160,768]{3,2,1,0:T(8,128)(2,1)}), bf16[8,2,160,768]{3,2,1,0:T(8,128)(2,1)}, u32[]{:S(2)}, u32[]{:S(2)}) async-start(bf16[8,2,160,768]{3,2,1,0:T(8,128)(2,1)} %pad_maximum_fusion), calls=%async_computation.1 | async-start | bytes 7864320 | tf_op jit(solution)/shard_map/all_to_all | solution.py:387
  84.7 44.9 %all-gather.5.cloned.1.call-start = ((), (), s32[]{:S(2)}) async-start(), calls=%async_computation.13 | async-start | bytes 1548288 | tf_op jit(solution)/shard_map/all_gather | solution.py:442
  99.9 84.8 %collective-permute-start.7 = (bf16[192,1024]{1,0:T(8,128)(2,1)}, bf16[192,1024]{1,0:T(8,128)(2,1)S(1)}, u32[]{:S(2)}, u32[]{:S(2)}) collective-permute-start(bf16[192,1024]{1,0:T(8,128)(2,1)} %get-tuple-element.75.o_ref), channel_id=1, source_target_pairs={{0,3},{1,0},{2,1},{3,2},{4,7},{5,4},{6,5},{7,6},{8,11},{9,8},{10,9... | collective-permute-start | bytes 1179656 | tf_op jit(solution)/shard_map/ppermute | solution.py:482
  100.3 84.5 %collective-permute-start.5 = (bf16[192,1024]{1,0:T(8,128)(2,1)}, bf16[192,1024]{1,0:T(8,128)(2,1)S(1)}, u32[]{:S(2)}, u32[]{:S(2)}) collective-permute-start(bf16[192,1024]{1,0:T(8,128)(2,1)} %get-tuple-element.75.o_ref), channel_id=1, source_target_pairs={{0,1},{1,2},{2,3},{3,0},{4,5},{5,6},{6,7},{7,4},{8,9},{9,10},{10,1... | collective-permute-start | bytes 1179656 | tf_op jit(solution)/shard_map/ppermute | solution.py:482
  102.0 84.3 %collective-permute-start.6 = (bf16[192,1024]{1,0:T(8,128)(2,1)}, bf16[192,1024]{1,0:T(8,128)(2,1)}, u32[]{:S(2)}, u32[]{:S(2)}) collective-permute-start(bf16[192,1024]{1,0:T(8,128)(2,1)} %get-tuple-element.75.o_ref), channel_id=1, source_target_pairs={{0,2},{1,3},{2,0},{3,1},{4,6},{5,7},{6,4},{7,5},{8,10},{9,11},{10,... | collective-permute-start | bytes 1179656 | tf_op jit(solution)/shard_map/ppermute | solution.py:482
  135.6 46.2 %copy-start.37 = (s32[320]{0:T(512)S(1)}, s32[320]{0:T(512)}, u32[]{:S(2)}) copy-start(s32[320]{0:T(512)} %iota_add_fusion.1) | copy-start | bytes 3844
  135.6 50.6 %copy-start.14 = (bf16[192,1024]{1,0:T(8,128)(2,1)S(1)}, bf16[192,1024]{1,0:T(8,128)(2,1)}, u32[]{:S(2)}) copy-start(bf16[192,1024]{1,0:T(8,128)(2,1)} %get-tuple-element.75.o_ref) | copy-start | bytes 1179652
  135.6 55.9 %all-to-all-start.2 = ((bf16[8,2,192,512]{3,2,1,0:T(8,128)(2,1)}), bf16[8,2,192,512]{3,2,1,0:T(8,128)(2,1)}, u32[]{:S(2)}, u32[]{:S(2)}) async-start(bf16[8,2,192,512]{3,2,1,0:T(8,128)(2,1)} %param.25), calls=%async_computation.2 | async-start | bytes 6291456 | tf_op jit(solution)/shard_map/all_to_all | solution.py:463
  140.9 43.8 %copy-start.31 = (s32[1024]{0:T(1024)}, s32[1024]{0:T(1024)S(1)}, u32[]{:S(2)}) copy-start(s32[1024]{0:T(1024)S(1)} %get-tuple-element.202) | copy-start | bytes 12292
  140.9 49.0 %copy-start.29 = (s32[1024]{0:T(1024)}, s32[1024]{0:T(1024)S(1)}, u32[]{:S(2)}) copy-start(s32[1024]{0:T(1024)S(1)} %get-tuple-element.201) | copy-start | bytes 12292
  199.2 28.8 %all-to-all-start.3 = ((bf16[8,1,160,768]{3,2,1,0:T(8,128)(2,1)}), bf16[8,1,160,768]{3,2,1,0:T(8,128)(2,1)}, u32[]{:S(2)}, u32[]{:S(2)}) async-start(bf16[8,1,160,768]{3,2,1,0:T(8,128)(2,1)} %bitcast.112), calls=%async_computation.3 | async-start | bytes 3932160 | tf_op jit(solution)/shard_map/all_to_all | solution.py:387
  228.0 32.0 %all-to-all-start.4 = ((bf16[8,1,160,768]{3,2,1,0:T(8,128)(2,1)}), bf16[8,1,160,768]{3,2,1,0:T(8,128)(2,1)}, u32[]{:S(2)}, u32[]{:S(2)}) async-start(bf16[8,1,160,768]{3,2,1,0:T(8,128)(2,1)} %bitcast.111), calls=%async_computation.4 | async-start | bytes 3932160 | tf_op jit(solution)/shard_map/all_to_all | solution.py:387
  232.5 66.5 %all-gather.7.cloned.1.call-start = ((), (), s32[]{:S(2)}) async-start(), calls=%async_computation.14 | async-start | bytes 2654208 | tf_op jit(solution)/shard_map/all_gather | solution.py:503
  260.0 29.1 %all-to-all-start.5 = ((bf16[8,1,160,768]{3,2,1,0:T(8,128)(2,1)}), bf16[8,1,160,768]{3,2,1,0:T(8,128)(2,1)}, u32[]{:S(2)}, u32[]{:S(2)}) async-start(bf16[8,1,160,768]{3,2,1,0:T(8,128)(2,1)} %get-tuple-element.101), calls=%async_computation.5 | async-start | bytes 3932160 | tf_op jit(solution)/shard_map/all_to_all | solution.py:387
  289.1 31.0 %all-to-all-start.6 = ((bf16[8,1,160,768]{3,2,1,0:T(8,128)(2,1)}), bf16[8,1,160,768]{3,2,1,0:T(8,128)(2,1)}, u32[]{:S(2)}, u32[]{:S(2)}) async-start(bf16[8,1,160,768]{3,2,1,0:T(8,128)(2,1)} %get-tuple-element.102), calls=%async_computation.6 | async-start | bytes 3932160 | tf_op jit(solution)/shard_map/all_to_all | solution.py:387
  359.7 28.7 %all-to-all-start.8 = ((bf16[8,1,160,768]{3,2,1,0:T(8,128)(2,1)}), bf16[8,1,160,768]{3,2,1,0:T(8,128)(2,1)}, u32[]{:S(2)}, u32[]{:S(2)}) async-start(bf16[8,1,160,768]{3,2,1,0:T(8,128)(2,1)} %get-tuple-element.108), calls=%async_computation.8 | async-start | bytes 3932160 | tf_op jit(solution)/shard_map/all_to_all | solution.py:387
  364.1 73.0 %all-reduce.5.cloned.1.call-start = ((), (), s32[]{:S(2)}) async-start(), calls=%async_computation.15 | async-start | bytes 3145728 | tf_op jit(solution)/shard_map/psum | solution.py:561
  388.4 62.0 %all-to-all-start.9 = ((bf16[8,1,160,768]{3,2,1,0:T(8,128)(2,1)}), bf16[8,1,160,768]{3,2,1,0:T(8,128)(2,1)}, u32[]{:S(2)}, u32[]{:S(2)}) async-start(bf16[8,1,160,768]{3,2,1,0:T(8,128)(2,1)} %get-tuple-element.112), calls=%async_computation.9 | async-start | bytes 3932160 | tf_op jit(solution)/shard_map/all_to_all | solution.py:387
  475.7 20.8 %collective-permute-start.8 = (bf16[384,1024]{1,0:T(8,128)(2,1)}, bf16[384,1024]{1,0:T(8,128)(2,1)}, u32[]{:S(2)}, u32[]{:S(2)}) collective-permute-start(bf16[384,1024]{1,0:T(8,128)(2,1)} %get-tuple-element.211), channel_id=1, source_target_pairs={{4,0},{8,4},{12,8},{5,1},{9,5},{13,9},{6,2},{10,6},{14,10},{7,3},{... | collective-permute-start | bytes 2359304 | tf_op jit(solution)/shard_map/ppermute | solution.py:593
  477.0 46.0 %collective-permute-start.9 = (bf16[384,1024]{1,0:T(8,128)(2,1)}, bf16[384,1024]{1,0:T(8,128)(2,1)}, u32[]{:S(2)}, u32[]{:S(2)}) collective-permute-start(bf16[384,1024]{1,0:T(8,128)(2,1)} %get-tuple-element.212), channel_id=1, source_target_pairs={{8,0},{12,4},{9,1},{13,5},{10,2},{14,6},{11,3},{15,7},{24,16},{28,... | collective-permute-start | bytes 2359304 | tf_op jit(solution)/shard_map/ppermute | solution.py:593
  478.3 54.5 %all-to-all-start.10 = ((bf16[4,2,192,512]{3,2,1,0:T(8,128)(2,1)}), bf16[4,2,192,512]{3,2,1,0:T(8,128)(2,1)}, u32[]{:S(2)}, u32[]{:S(2)}) async-start(bf16[4,2,192,512]{3,2,1,0:T(8,128)(2,1)} %pad_maximum_fusion.3), calls=%async_computation.10 | async-start | bytes 3145728 | tf_op jit(solution)/shard_map/all_to_all | solution.py:532
  532.8 85.9 %all-to-all-start.11 = ((bf16[4,2,2,192,512]{4,3,2,1,0:T(8,128)(2,1)}), bf16[4,2,2,192,512]{4,3,2,1,0:T(8,128)(2,1)}, u32[]{:S(2)}, u32[]{:S(2)}) async-start(bf16[4,2,2,192,512]{4,3,2,1,0:T(8,128)(2,1)} %pad_maximum_fusion.1), calls=%async_computation.11 | async-start | bytes 6291456 | tf_op jit(solution)/shard_map/all_to_all | solution.py:532
  537.5 72.9 %all-reduce.7.cloned.1.call-start = ((), (), s32[]{:S(2)}) async-start(), calls=%async_computation.16 | async-start | bytes 3145728 | tf_op jit(solution)/shard_map/psum | solution.py:583
  538.1 143.1 %all-reduce.9.cloned.1.call-start = ((), (), s32[]{:S(2)}) async-start(), calls=%async_computation.17 | async-start | bytes 3145728 | tf_op jit(solution)/shard_map/psum | solution.py:602
  618.7 22.3 %all-to-all-start.12 = ((bf16[8,96,786]{2,1,0:T(8,128)(2,1)}), bf16[8,96,786]{2,1,0:T(8,128)(2,1)}, u32[]{:S(2)}, u32[]{:S(2)}) async-start(bf16[8,96,786]{2,1,0:T(8,128)(2,1)} %bitcast.103), calls=%async_computation.12 | async-start | bytes 2752512 | tf_op jit(solution)/shard_map/all_to_all | solution.py:320
  642.6 41.5 %copy-start.1 = (f32[1024,768]{1,0:T(8,128)S(1)}, f32[1024,768]{1,0:T(8,128)}, u32[]{:S(2)}) copy-start(f32[1024,768]{1,0:T(8,128)} %copy-done) | copy-start | bytes 9437188
  (49 other events, 281.1 us)
Sparse Core Ops, SparseCore 0:
  88.0 41.5 all-gather.4
  235.8 32.4 all-gather.6
  367.8 69.1 all-reduce.4
  540.9 69.4 all-reduce.6
  612.6 68.5 all-reduce.8

commit v3 on v2

--- a/solution.py
+++ b/solution.py
@@ -118,13 +118,14 @@
             dq_ref[h, here] = dq * 0.125
 
 
-def whole(shape):
-    return pl.BlockSpec(shape, lambda n, lo: (0, 0))
-
-
-def attn_forward(lo, q_t, k_t, v_t, doc, shift):
+def whole(shape, at=0):
+    return pl.BlockSpec(shape, lambda n, lo: (at, 0))
+
+
+def attn_forward(lo, q_t, kv_t, doc, shift):
     heads, rows = q_t.shape[0] // HD, q_t.shape[1]
-    ins = (q_t, k_t, v_t, doc)
+    half = (q_t.shape[0], kv_t.shape[1])
+    ins = (q_t, kv_t, kv_t, doc)
     outs = (
         jax.ShapeDtypeStruct(q_t.shape, BF),
         jax.ShapeDtypeStruct((heads, rows), F32),
@@ -135,19 +136,21 @@
         grid_spec=pltpu.PrefetchScalarGridSpec(
             num_scalar_prefetch=1,
             grid=(1,),
-            in_specs=[whole(v.shape) for v in ins],
+            in_specs=[whole(q_t.shape), whole(half), whole(half, 1)]
+            + [whole(v.shape) for v in ins[3:]],
             out_specs=[whole(v.shape) for v in outs],
         ),
         name="attn_fwd",
     )(lo, *ins)
 
 
-def attn_backward(lo, q_t, k_t, v_t, o_t, do_t, lse, doc, shift):
-    ins = (q_t, k_t, v_t, o_t, do_t, lse, doc)
+def attn_backward(lo, q_t, kv_t, o_t, do_t, lse, doc, shift):
+    half = (q_t.shape[0], kv_t.shape[1])
+    ins = (q_t, kv_t, kv_t, o_t, do_t, lse, doc)
     outs = (
         jax.ShapeDtypeStruct(q_t.shape, F32),
-        jax.ShapeDtypeStruct(k_t.shape, F32),
-        jax.ShapeDtypeStruct(k_t.shape, F32),
+        jax.ShapeDtypeStruct(half, F32),
+        jax.ShapeDtypeStruct(half, F32),
     )
     return pl.pallas_call(
         functools.partial(attn_bwd_kernel, shift=shift),
@@ -155,7 +158,8 @@
         grid_spec=pltpu.PrefetchScalarGridSpec(
             num_scalar_prefetch=1,
             grid=(1,),
-            in_specs=[whole(v.shape) for v in ins],
+            in_specs=[whole(q_t.shape), whole(half), whole(half, 1)]
+            + [whole(v.shape) for v in ins[3:]],
             out_specs=[whole(v.shape) for v in outs],
         ),
         name="attn_bwd",
@@ -164,8 +168,8 @@
 
 def ffn_kernel(*refs, gated):
     if gated:
-        first_ref, x_ref, g_ref, other_ref, router_ref, win_ref, wout_ref = refs[:7]
-        y_ref, dx_ref, gin_ref, gout_ref, grouter_ref, acc_in, acc_out, acc_router = refs[7:]
+        first_ref, x_ref, g_ref, router_ref, win_ref, wout_ref = refs[:6]
+        y_ref, dx_ref, gin_ref, gout_ref, grouter_ref, acc_in, acc_out, acc_router = refs[6:]
     else:
         x_ref, g_ref, win_ref, wout_ref = refs[:4]
         y_ref, dx_ref, gin_ref, gout_ref, acc_in, acc_out = refs[4:]
@@ -184,7 +188,7 @@
             acc_router[...] = jnp.zeros_like(acc_router)
 
     x = x_ref[...].reshape(src * rows, width)
-    g = g_ref[...].reshape(src * rows, width)
+    g = g_ref[..., :width].reshape(src * rows, width)
     w_gate = win_ref[0, 0]
     w_up = win_ref[0, 1]
     w_out = wout_ref[0]
@@ -199,7 +203,9 @@
         logits = mm(x, router, 1, 0)
         ids = lax.broadcasted_iota(jnp.int32, logits.shape, 1)
         here = ids == first_ref[0] + expert
-        there = ids == other_ref[...].reshape(src * rows, 1)
+        marks = g_ref[..., width : width + 128].reshape(src * rows, 128)
+        other = marks[:, :1].astype(F32).astype(jnp.int32) - 1 - (first_ref[0] + expert)
+        there = ids == other
         apart = jnp.sum(
             jnp.where(here, logits, 0.0) - jnp.where(there, logits, 0.0), axis=1, keepdims=True
         )
@@ -241,7 +247,7 @@
     gated = routing is not None
     block = math.gcd(sources, block)
     big = pl.BlockSpec((block, 1, rows, width), lambda e, s, *_: (s, e, 0, 0))
-    big_at = pl.BlockSpec((block, 1, rows, width), lambda e, s, *_: (s, at + e, 0, 0))
+    big_at = pl.BlockSpec((block, 1, rows, g.shape[3]), lambda e, s, *_: (s, at + e, 0, 0))
     w_in_at = pl.BlockSpec((1, 2, width, units), lambda e, s, *_: (at + e, 0, 0, 0))
     w_out_at = pl.BlockSpec((1, width, units), lambda e, s, *_: (at + e, 0, 0))
     cut = width // parts
@@ -259,11 +265,10 @@
     out_specs = [big, big, g_in_spec, g_out_spec]
     scratch = [pltpu.VMEM((2, width, units), F32), pltpu.VMEM((width, units), F32)]
     if gated:
-        first, other, router = routing
+        first, router = routing
         router_spec = pl.BlockSpec(router.shape, lambda e, s, *_: (0, 0))
-        ins = [first] + ins + [other, router]
-        thin = pl.BlockSpec((block, 1, rows, 1), lambda e, s, *_: (s, at + e, 0, 0))
-        in_specs += [thin, router_spec]
+        ins = [first] + ins + [router]
+        in_specs.append(router_spec)
         outs.append(jax.ShapeDtypeStruct(router.shape, F32))
         out_specs.append(router_spec)
         scratch.append(pltpu.VMEM(router.shape, F32))
@@ -395,16 +400,17 @@
         for n in range(own)
     ]
     first = lax.axis_index(expert_axes) * own
-    my_slots = first * capacity + jnp.arange(own * capacity, dtype=jnp.int32)
+    sums = (jnp.sum(my_routes, axis=1, keepdims=True) + 1).astype(BF)
+    marked = jnp.concatenate([grad_low, jnp.pad(sums, ((0, 0), (0, 127)))], axis=1)
     to_slot = [
         ((place[None, :, 0] == ids[:, None]) | (place[None, :, 1] == ids[:, None])).astype(BF)
         for ids in block_ids
     ]
     slot_g = jnp.stack(
         [
-            jnp.dot(hits, grad_low, preferred_element_type=F32)
+            jnp.dot(hits, marked, preferred_element_type=F32)
             .astype(BF)
-            .reshape(owners, capacity, width)
+            .reshape(owners, capacity, width + 128)
             for hits in to_slot
         ],
         axis=1,
@@ -436,7 +442,6 @@
         pieces.insert(0, lax.ppermute(kv_t, "ctx", links))
     kv_win = jnp.concatenate(pieces, axis=1)
     kv_win, slot_g, second_w, eout = tie(kv_win, slot_g, second_w, eout)
-    k_win, v_win = kv_win[:heads_cols], kv_win[heads_cols:]
 
     got_g = swap(slot_g)
     second_full = lax.all_gather(second_w, DC, axis=0, tiled=True)
@@ -457,30 +462,13 @@
     ) - (row_start - shift)
     lo = jnp.maximum(doc[::BQ], 0) // BK
     doc = doc[None, :]
-    att_t, lse = attn_forward(lo, q_t, k_win, v_win, doc, shift)
-    place, expert_in, lse, got_g = tie(place, expert_in, lse, got_g)
+    att_t, lse = attn_forward(lo, q_t, kv_win, doc, shift)
+    expert_in, lse, got_g = tie(expert_in, lse, got_g)
     if spread:
         ein = lax.all_to_all(expert_in, "ctx", split_axis=0, concat_axis=2, tiled=True)
     else:
         ein = lax.all_gather(expert_in, "ctx", axis=2, tiled=True)
-    pairs = lax.all_gather(
-        jnp.stack([place[:, 0], place[:, 1], my_routes[:, 1], my_routes[:, 0]]),
-        expert_axes,
-        axis=0,
-    )
-    slot_other = (
-        jnp.sum(
-            jnp.where(
-                pairs[:, :2, None, :] == my_slots[None, None, :, None],
-                pairs[:, 2:, None, :] + 1,
-                0,
-            ),
-            axis=(1, 3),
-        )
-        - 1
-    ).reshape(owners, own, capacity, 1)
     att_parts = [att_t] + [lax.ppermute(att_t, "tensor", links) for links in rings]
-    att_parts[-1], slot_other = tie(att_parts[-1], slot_other)
     branch = jnp.einsum(
         "cl,dc->ld", jnp.concatenate(att_parts, axis=0), out_all, preferred_element_type=F32
     )
@@ -511,7 +499,7 @@
             eout,
             4,
             ctx_count,
-            (jnp.reshape(first + n, (1,)).astype(jnp.int32), slot_other, router_wide),
+            (jnp.reshape(first + n, (1,)).astype(jnp.int32), router_wide),
             n,
         )
         ys.append(y)
@@ -559,17 +547,15 @@
     dn2_part = at_tokens(back_dx, sh_dx)
     dn2_low = dn2_part.astype(BF)
     dn2 = lax.psum(dn2_low, "tensor")
-    sh_grad, dn2_low = tie(jnp.concatenate([sh_gin[:, 0], sh_gout], axis=1), dn2_low)
-    shared_parts = lax.all_to_all(sh_grad, DC, split_axis=0, concat_axis=0, tiled=True)
-    ys[0], shared_parts = tie(ys[0], shared_parts)
-    total_shared = jnp.sum(shared_parts.astype(F32), axis=0)
+    ys[0], dn2_low = tie(ys[0], dn2_low)
     back_y = []
     for y in ys:
         if back_y:
             y, back_y[-1] = tie(y, back_y[-1])
         back_y.append(swap(y).reshape(-1, width))
-    g_eout, back_y[-1] = tie(g_eout, back_y[-1])
-    grad_eout = to_owner(g_eout)
+    sh_grad, back_y[-1] = tie(jnp.concatenate([sh_gin[:, 0], sh_gout], axis=1), back_y[-1])
+    shared_parts = lax.all_to_all(sh_grad, DC, split_axis=0, concat_axis=0, tiled=True)
+    dn2, back_y[-1] = tie(dn2, back_y[-1])
     dn2 = dn2.astype(F32)
     gain2_part = jnp.sum(dn2_part * n2, axis=0)
 
@@ -583,7 +569,7 @@
     ffn_total = lax.psum(ffn_low, "tensor")
 
     dq_t, dk_win, dv_win = attn_backward(
-        lo, q_t, k_win, v_win, att_t, datt_t, lse, doc, shift
+        lo, q_t, kv_win, att_t, datt_t, lse, doc, shift
     )
     dkv_win = jnp.concatenate([dk_win, dv_win], axis=0)
     dkv = dkv_win[:, shift:]
@@ -594,8 +580,9 @@
     dq_raw = half_turn(dq_t, cos_t, -sin_t)
     dk_raw = half_turn(dkv[:heads_cols], cos_t, -sin_t)
     draw_t = jnp.concatenate([dq_raw, dk_raw, dkv[heads_cols:]], axis=0).astype(BF)
-    g_ein, draw_t, grad_eout = tie(g_ein, draw_t, grad_eout)
-    grad_ein = to_owner(g_ein)
+    g_eout, draw_t, shared_parts = tie(g_eout, draw_t, shared_parts)
+    total_shared = jnp.sum(shared_parts.astype(F32), axis=0)
+    grad_eout = to_owner(g_eout)
     dn1_part = jnp.einsum("cl,dc->ld", draw_t, qkv_full, preferred_element_type=F32)
     dn1_low, ffn_total = lax.optimization_barrier((dn1_part.astype(BF), ffn_total))
     layer_out = (resid + ffn_total.astype(F32)).astype(BF)
@@ -610,8 +597,10 @@
         Layout((0, 1)),
     )
     small = jnp.concatenate([router_part, gain1_part[:, None], gain2_part[:, None]], axis=1).astype(BF)
-    mixed, grad_ein = tie(jnp.concatenate([grad_qkv, grad_outw, small], axis=1), grad_ein)
+    mixed, grad_eout = tie(jnp.concatenate([grad_qkv, grad_outw, small], axis=1), grad_eout)
     tail = own_sum(mixed, 0)
+    g_ein, tail = tie(g_ein, tail)
+    grad_ein = to_owner(g_ein)
     small = lax.psum(tail[:, 4 * heads_cols :], "tensor")
     total_qkv = tail[:, : 3 * heads_cols].reshape(-1, 3, heads_cols).transpose(1, 0, 2)
     total_outw = tail[:, 3 * heads_cols : 4 * heads_cols]

time: 704 us -> 710 us (level)
  waiting for transfers between devices: 245 us -> 300 us
  blocking collectives: 105 us -> 60.6 us
  matrix products: 74.6 us -> 64.3 us
    all_to_all x7 -> x6, waiting for transfers between devices: 55.1 us -> 96.3 us  [swap(): lax.all_to_all(values, expert_axes, split_axis=0, concat_axis=0, tiled=True)]
    all_gather x1 -> x0, blocking collectives: 40.7 us -> none  [shards(): lax.all_gather(jnp.stack([place[:, 0], place[:, 1], my_routes[:, 1], my_r...]
    ppermute x3, waiting for transfers between devices: 0.01 us -> 33.3 us  [shards(): lax.ppermute(att_t, 'tensor', links)]
    all_gather x1, waiting for transfers between devices: 27.4 us -> 0.01 us  [shards(): second_full = lax.all_gather(second_w, DC, axis=0, tiled=True)]
    all_to_all x0 -> x1, starting transfers between devices: none -> 14.1 us  [shards(): lax.all_to_all(sh_grad, DC, split_axis=0, concat_axis=0, tiled=True)]
    psum x1, waiting for transfers between devices: 19.2 us -> 32.7 us  [shards(): dn1 = lax.psum(dn1_low, 'tensor')]
    psum x1, waiting for transfers between devices: 62.2 us -> 48.9 us  [shards(): ffn_total = lax.psum(ffn_low, 'tensor')]
    ppermute x2, waiting for transfers between devices: 26.5 us -> 35.2 us  [shards(): dkv = dkv + lax.ppermute(piece.astype(BF), 'ctx', links).astype(F32)]
  transfers between devices with their start and end apart: 27 -> 27, of which waited for: 12 -> 13; matrix products, arithmetic and copies ran while one was open for 18% -> 17% of each run, Pallas kernels for 8% -> 8%
where the time goes in v3:
time: 710 us; the launch traced here: 704 us
  waiting for transfers between devices  300 us (42%)
  starting transfers between devices  86.8 us (12%)
  Pallas kernels  71.3 us (10%)
  other arithmetic  65.4 us (9%)
  matrix products  64.3 us (9%)
  blocking collectives  60.6 us (9%)
  local copies, waits for them, and re-layouts  41.5 us (6%)
  between operations  14.8 us (2%)
    all_to_all x6, waiting for transfers between devices, swap(): lax.all_to_all(values, expert_axes, split_axis=0, concat_axis=0, tiled=True)  96.3 us
    pallas_call x3, Pallas kernels, ffn(): pl.pallas_call(functools.partial(ffn_kernel, gated=gated), out_shape=outs...  49.4 us
    psum x1, waiting for transfers between devices, shards(): ffn_total = lax.psum(ffn_low, 'tensor')  48.9 us
    psum x1, waiting for transfers between devices, shards(): dn2 = lax.psum(dn2_low, 'tensor')  47.6 us
    ppermute x2, waiting for transfers between devices, shards(): dkv = dkv + lax.ppermute(piece.astype(BF), 'ctx', links).astype(F32)  35.2 us
    ppermute x3, waiting for transfers between devices, shards(): lax.ppermute(att_t, 'tensor', links)  33.3 us
    psum x1, waiting for transfers between devices, shards(): dn1 = lax.psum(dn1_low, 'tensor')  32.7 us
    all_to_all x1, blocking collectives, swap(): lax.all_to_all(values, expert_axes, split_axis=0, concat_axis=0, tiled=True)  29.4 us
  transfers between devices with their start and end apart: 27, of which 13 were waited for; matrix products, arithmetic and copies ran while one was open for 17% of the time, Pallas kernels for 8%

profile of v3, /device:TPU:0, one launch (start us, length us, event | category | flops | bytes accessed | tf_op | source)
XLA Modules:
  0.0 704.4 jit_solution(414570342858487682)
XLA Ops:
  9.2 12.3 %all_gather.9 = bf16[768,577]{1,0:T(8,128)(2,1)S(1)} all-gather(bf16[96,577]{1,0:T(8,128)(2,1)S(1)} %copy.84), channel_id=1, replica_groups=mesh['dp'=2,'ctx'=4,'tensor'=4] {'dp','ctx'}, dimensions={0}, use_global_device_ids=true | all-gather | bytes 997056 | tf_op jit(solution)/shard_map/all_gather | solution.py:370
  48.0 5.0 fusion.72
  62.4 5.1 fusion.18
  81.4 4.7 all-to-all-start.1
  88.5 8.4 %attn_fwd.1 = (bf16[192,1024]{1,0:T(8,128)(2,1)}, f32[3,1024]{1,0:T(4,128)}) custom-call(s32[2]{0:T(128)} %and_select_fusion.lo_ref, bf16[192,1024]{1,0:T(8,128)(2,1)} %bitcast.102, bf16[384,3072]{1,0:T(8,128)(2,1)} %maximum_maximum_fusion.k_ref.v_ref, bf16[384,3072]{1,0:T(8,128)(2,1)} %maximum_maximum_fusion.k_ref.v_ref, s32[1,1024]{1,0:T(1,128)} %bitcast.123), custom_call_target="tpu_custom_call" | custom-call | tf_op jit(solution)/shard_map/attn_fwd/pallas_call | solution.py:133
  96.9 47.1 %all-to-all-done.1.refs_2_ = bf16[8,2,160,896]{3,2,1,0:T(8,128)(2,1)} async-done(((bf16[8,2,160,896]{3,2,1,0:T(8,128)(2,1)}), bf16[8,2,160,896]{3,2,1,0:T(8,128)(2,1)}, u32[]{:S(2)}, u32[]{:S(2)}) %all-to-all-start.1) | async-done | bytes 4587552 | tf_op jit(solution)/shard_map/all_to_all | solution.py:392
  144.0 4.8 all-to-all-start.2
  152.4 8.0 %collective-permute-done.7 = bf16[192,1024]{1,0:T(8,128)(2,1)S(1)} collective-permute-done((bf16[192,1024]{1,0:T(8,128)(2,1)S(1)}, bf16[192,1024]{1,0:T(8,128)(2,1)S(1)}, u32[]{:S(2)}, u32[]{:S(2)}) %collective-permute-start.7) | collective-permute-done | bytes 393248 | tf_op jit(solution)/shard_map/ppermute | solution.py:471
  160.4 25.3 %collective-permute-done.6 = bf16[192,1024]{1,0:T(8,128)(2,1)S(1)} collective-permute-done((bf16[192,1024]{1,0:T(8,128)(2,1)S(1)}, bf16[192,1024]{1,0:T(8,128)(2,1)S(1)}, u32[]{:S(2)}, u32[]{:S(2)}) %collective-permute-start.6) | collective-permute-done | bytes 393248 | tf_op jit(solution)/shard_map/ppermute | solution.py:471
  199.4 4.7 all-to-all-start.3
  204.1 5.2 fusion.20
  209.3 19.1 %all-to-all-done.3.refs_1_ = bf16[8,1,160,768]{3,2,1,0:T(8,128)(2,1)} async-done(((bf16[8,1,160,768]{3,2,1,0:T(8,128)(2,1)}), bf16[8,1,160,768]{3,2,1,0:T(8,128)(2,1)}, u32[]{:S(2)}, u32[]{:S(2)}) %all-to-all-start.3) | async-done | bytes 1966112 | tf_op jit(solution)/shard_map/all_to_all | solution.py:392
  235.4 18.1 %ffn_experts.2 = (bf16[8,1,160,768]{3,2,1,0:T(8,128)(2,1)}, bf16[8,1,160,768]{3,2,1,0:T(8,128)(2,1)}, bf16[4,1,2,192,512]{4,3,2,1,0:T(8,128)(2,1)}, bf16[4,1,192,512]{3,2,1,0:T(8,128)(2,1)}, f32[768,128]{1,0:T(8,128)}) custom-call(s32[1]{0:T(128)} %bitcast.21.refs_0_, bf16[8,1,160,768]{3,2,1,0:T(8,128)(2,1)} %all-to-all-done.3.refs_1_, ...), custom_call_target="tpu_custom_call" | custom-call | tf_op jit(solution)/shard_map/ffn_experts/pallas_call | solution.py:275
  253.5 6.9 all-to-all-done.4.refs_1_
  265.0 18.2 %ffn_experts.3 = (bf16[8,1,160,768]{3,2,1,0:T(8,128)(2,1)}, bf16[8,1,160,768]{3,2,1,0:T(8,128)(2,1)}, bf16[4,1,2,192,512]{4,3,2,1,0:T(8,128)(2,1)}, bf16[4,1,192,512]{3,2,1,0:T(8,128)(2,1)}, f32[768,128]{1,0:T(8,128)}) custom-call(s32[1]{0:T(128)} %bitcast.27.refs_0_, bf16[8,1,160,768]{3,2,1,0:T(8,128)(2,1)} %all-to-all-done.4.refs_1_, ...), custom_call_target="tpu_custom_call" | custom-call | tf_op jit(solution)/shard_map/ffn_experts/pallas_call | solution.py:275
  283.2 6.1 all-to-all-done.5
  289.3 4.8 all-to-all-start.6
  294.1 5.4 fusion.14
  304.3 13.1 %ffn_shared.1 = (bf16[4,1,256,768]{3,2,1,0:T(8,128)(2,1)}, bf16[4,1,256,768]{3,2,1,0:T(8,128)(2,1)}, bf16[8,1,2,96,512]{4,3,2,1,0:T(8,128)(2,1)}, bf16[8,1,96,512]{3,2,1,0:T(8,128)(2,1)}) custom-call(bf16[4,1,256,768]{3,2,1,0:T(8,128)(2,1)} %bitcast.98, bf16[4,1,256,768]{3,2,1,0:T(8,128)(2,1)} %bitcast.94, ...), custom_call_target="tpu_custom_call" | custom-call | tf_op jit(solution)/shard_map/ffn_shared/pallas_call | solution.py:275
  318.4 6.4 fusion.95
  324.8 29.4 %all_to_all.91 = bf16[8,1,160,768]{3,2,1,0:T(8,128)(2,1)} all-to-all(bf16[8,1,160,768]{3,2,1,0:T(8,128)(2,1)} %get-tuple-element.101), channel_id=1, replica_groups=mesh['dp'=2,'ctx'=4,'tensor'=4] {'dp','ctx'}, dimensions={0} | all-to-all | bytes 3932160 | tf_op jit(solution)/shard_map/all_to_all | solution.py:392
  366.8 16.1 %all-to-all-done.8 = bf16[8,1,160,768]{3,2,1,0:T(8,128)(2,1)} async-done(((bf16[8,1,160,768]{3,2,1,0:T(8,128)(2,1)}), bf16[8,1,160,768]{3,2,1,0:T(8,128)(2,1)}, u32[]{:S(2)}, u32[]{:S(2)}) %all-to-all-start.8) | async-done | bytes 1966112 | tf_op jit(solution)/shard_map/all_to_all | solution.py:392
  382.9 47.6 %all-reduce.6.cloned.1.call-done = bf16[1024,768]{1,0:T(8,128)(2,1)} async-done(((bf16[1024,768]{1,0:T(8,128)(2,1)}), bf16[1024,768]{1,0:T(8,128)(2,1)}) %all-reduce.6.cloned.1.call-update) | async-done | bytes 1572880 | tf_op jit(solution)/shard_map/psum | solution.py:549
  437.9 5.2 fusion.32
  446.6 13.4 %attn_bwd.1 = (f32[192,1024]{1,0:T(8,128)}, f32[192,3072]{1,0:T(8,128)}, f32[192,3072]{1,0:T(8,128)}) custom-call(s32[2]{0:T(128)} %and_select_fusion.lo_ref, bf16[192,1024]{1,0:T(8,128)(2,1)} %bitcast.103, bf16[384,3072]{1,0:T(8,128)(2,1)} %maximum_maximum_fusion.k_ref.v_ref, bf16[384,3072]{1,0:T(8,128)(2,1)} %maximum_maximum_fusion.k_ref.v_ref, ...), custom_call_target="tpu_custom_call" | custom-call | tf_op jit(solution)/shard_map/attn_bwd/pallas_call | solution.py:155
  463.3 14.1 %all-to-all-start.9 = ((bf16[8,3,96,512]{3,2,1,0:T(8,128)(2,1)}), bf16[8,3,96,512]{3,2,1,0:T(8,128)(2,1)}, u32[]{:S(2)}, u32[]{:S(2)}) async-start(bf16[8,3,96,512]{3,2,1,0:T(8,128)(2,1)} %pad_maximum_fusion.2), calls=%async_computation.9 | async-start | bytes 4718592 | tf_op jit(solution)/shard_map/all_to_all | solution.py:557
  487.6 35.2 %collective-permute-done.9 = bf16[384,1024]{1,0:T(8,128)(2,1)S(1)} collective-permute-done((bf16[384,1024]{1,0:T(8,128)(2,1)S(1)}, bf16[384,1024]{1,0:T(8,128)(2,1)S(1)}, u32[]{:S(2)}, u32[]{:S(2)}) %collective-permute-start.9) | collective-permute-done | bytes 786464 | tf_op jit(solution)/shard_map/ppermute | solution.py:579
  527.2 9.6 %all-to-all-start.10 = ((bf16[4,2,192,512]{3,2,1,0:T(8,128)(2,1)}), bf16[4,2,192,512]{3,2,1,0:T(8,128)(2,1)}, u32[]{:S(2)}, u32[]{:S(2)}) async-start(bf16[4,2,192,512]{3,2,1,0:T(8,128)(2,1)} %pad_maximum_fusion.3), calls=%async_computation.10 | async-start | bytes 3145728 | tf_op jit(solution)/shard_map/all_to_all | solution.py:520
  561.3 48.9 %all-reduce.8.cloned.1.call-done = bf16[1024,768]{1,0:T(8,128)(2,1)} async-done(((bf16[1024,768]{1,0:T(8,128)(2,1)}), bf16[1024,768]{1,0:T(8,128)(2,1)}) %all-reduce.8.cloned.1.call-update) | async-done | bytes 1572880 | tf_op jit(solution)/shard_map/psum | solution.py:569
  630.5 18.9 %psum.31 = f32[96,18]{1,0:T(8,128)S(1)} all-reduce(f32[96,18]{1,0:T(8,128)S(1)} %slice.148), channel_id=1, replica_groups=mesh['dp'=2,'ctx'=4,'tensor'=4] {'tensor'}, use_global_device_ids=true, to_apply=%region_13.14 | all-reduce | flops 1728 | bytes 13824 | tf_op jit(solution)/shard_map/psum | solution.py:604
  649.4 32.7 %all-reduce.10.cloned.1.call-done = bf16[1024,768]{1,0:T(8,128)(2,1)} async-done(((bf16[1024,768]{1,0:T(8,128)(2,1)}), bf16[1024,768]{1,0:T(8,128)(2,1)}) %all-reduce.10.cloned.1.call-update) | async-done | bytes 1572880 | tf_op jit(solution)/shard_map/psum | solution.py:589
  692.2 5.5 bitcast_convert_fusion
  (241 shorter events, 184.4 us)
Async XLA Ops:
  26.0 18.3 %copy-start.30 = (s32[1,1024,2]{1,2,0:T(2,128)S(1)}, s32[1,1024,2]{1,2,0:T(2,128)}, u32[]{:S(2)}) copy-start(s32[1,1024,2]{1,2,0:T(2,128)} %param.16) | copy-start | bytes 24580
  27.0 17.9 %copy-start.49 = (s32[1,1,2048]{2,1,0:T(1,128)S(1)}, s32[1,1,2048]{2,1,0:T(1,128)}, u32[]{:S(2)}) copy-start(s32[1,1,2048]{2,1,0:T(1,128)} %param.17) | copy-start | bytes 24580
  27.0 50.0 %collective-permute-start.1 = (bf16[384,1024]{1,0:T(8,128)(2,1)}, bf16[384,1024]{1,0:T(8,128)(2,1)}, u32[]{:S(2)}, u32[]{:S(2)}) collective-permute-start(bf16[384,1024]{1,0:T(8,128)(2,1)} %pad_maximum_fusion.5), channel_id=1, source_target_pairs={{0,4},{4,8},{8,12},{1,5},{5,9},{9,13},{2,6},{6,10},{10,14},{3,7},{... | collective-permute-start | bytes 2359304 | tf_op jit(solution)/shard_map/ppermute | solution.py:442
  30.3 46.7 %collective-permute-start = (bf16[384,1024]{1,0:T(8,128)(2,1)}, bf16[384,1024]{1,0:T(8,128)(2,1)}, u32[]{:S(2)}, u32[]{:S(2)}) collective-permute-start(bf16[384,1024]{1,0:T(8,128)(2,1)} %pad_maximum_fusion.5), channel_id=1, source_target_pairs={{0,8},{4,12},{1,9},{5,13},{2,10},{6,14},{3,11},{7,15},{16,24},{20,... | collective-permute-start | bytes 2359304 | tf_op jit(solution)/shard_map/ppermute | solution.py:442
  33.7 41.6 %collective-permute-start.2 = (bf16[96,192]{1,0:T(8,128)(2,1)}, bf16[96,192]{1,0:T(8,128)(2,1)}, u32[]{:S(2)}, u32[]{:S(2)}) collective-permute-start(bf16[96,192]{1,0:T(8,128)(2,1)} %param.20), channel_id=1, source_target_pairs={{0,1},{1,2},{2,3},{3,0},{4,5},{5,6},{6,7},{7,4},{8,9},{9,10},{10,1... | collective-permute-start | bytes 110600 | tf_op jit(solution)/shard_map/ppermute | solution.py:379
  35.3 40.0 %collective-permute-start.3 = (bf16[96,192]{1,0:T(8,128)(2,1)}, bf16[96,192]{1,0:T(8,128)(2,1)}, u32[]{:S(2)}, u32[]{:S(2)}) collective-permute-start(bf16[96,192]{1,0:T(8,128)(2,1)} %param.20), channel_id=1, source_target_pairs={{0,2},{1,3},{2,0},{3,1},{4,6},{5,7},{6,4},{7,5},{8,10},{9,11},{10,... | collective-permute-start | bytes 110600 | tf_op jit(solution)/shard_map/ppermute | solution.py:379
  37.9 37.4 %collective-permute-start.4 = (bf16[96,192]{1,0:T(8,128)(2,1)}, bf16[96,192]{1,0:T(8,128)(2,1)}, u32[]{:S(2)}, u32[]{:S(2)}) collective-permute-start(bf16[96,192]{1,0:T(8,128)(2,1)} %param.20), channel_id=1, source_target_pairs={{0,3},{1,0},{2,1},{3,2},{4,7},{5,4},{6,5},{7,6},{8,11},{9,8},{10,9... | collective-permute-start | bytes 110600 | tf_op jit(solution)/shard_map/ppermute | solution.py:379
  39.3 40.8 %all-to-all-start = ((bf16[8,192,512]{2,1,0:T(8,128)(2,1)}), bf16[8,192,512]{2,1,0:T(8,128)(2,1)S(1)}, u32[]{:S(2)}, u32[]{:S(2)}) async-start(bf16[8,192,512]{2,1,0:T(8,128)(2,1)} %param.26), calls=%async_computation | async-start | bytes 3145728 | tf_op jit(solution)/shard_map/all_to_all | solution.py:429
  81.4 62.7 %all-to-all-start.1 = ((bf16[8,2,160,896]{3,2,1,0:T(8,128)(2,1)}), bf16[8,2,160,896]{3,2,1,0:T(8,128)(2,1)}, u32[]{:S(2)}, u32[]{:S(2)}) async-start(bf16[8,2,160,896]{3,2,1,0:T(8,128)(2,1)} %pad_maximum_fusion), calls=%async_computation.1 | async-start | bytes 9175040 | tf_op jit(solution)/shard_map/all_to_all | solution.py:392
  86.1 65.1 %all-gather.3.cloned.1.call-start = ((), (), s32[]{:S(2)}) async-start(), calls=%async_computation.13 | async-start | bytes 1548288 | tf_op jit(solution)/shard_map/all_gather | solution.py:447
  144.0 47.7 %all-to-all-start.2 = ((bf16[8,2,192,512]{3,2,1,0:T(8,128)(2,1)}), bf16[8,2,192,512]{3,2,1,0:T(8,128)(2,1)}, u32[]{:S(2)}, u32[]{:S(2)}) async-start(bf16[8,2,192,512]{3,2,1,0:T(8,128)(2,1)} %param.25), calls=%async_computation.2 | async-start | bytes 6291456 | tf_op jit(solution)/shard_map/all_to_all | solution.py:468
  148.9 11.5 %collective-permute-start.7 = (bf16[192,1024]{1,0:T(8,128)(2,1)S(1)}, bf16[192,1024]{1,0:T(8,128)(2,1)S(1)}, u32[]{:S(2)}, u32[]{:S(2)}) collective-permute-start(bf16[192,1024]{1,0:T(8,128)(2,1)S(1)} %copy-done.14), channel_id=1, source_target_pairs={{0,3},{1,0},{2,1},{3,2},{4,7},{5,4},{6,5},{7,6},{8,11},{9,8},{10,9... | collective-permute-start | bytes 1179656 | tf_op jit(solution)/shard_map/ppermute | solution.py:471
  149.3 36.4 %collective-permute-start.6 = (bf16[192,1024]{1,0:T(8,128)(2,1)S(1)}, bf16[192,1024]{1,0:T(8,128)(2,1)S(1)}, u32[]{:S(2)}, u32[]{:S(2)}) collective-permute-start(bf16[192,1024]{1,0:T(8,128)(2,1)S(1)} %copy-done.14), channel_id=1, source_target_pairs={{0,2},{1,3},{2,0},{3,1},{4,6},{5,7},{6,4},{7,5},{8,10},{9,11},{10,... | collective-permute-start | bytes 1179656 | tf_op jit(solution)/shard_map/ppermute | solution.py:471
  151.0 35.4 %collective-permute-start.5 = (bf16[192,1024]{1,0:T(8,128)(2,1)S(1)}, bf16[192,1024]{1,0:T(8,128)(2,1)}, u32[]{:S(2)}, u32[]{:S(2)}) collective-permute-start(bf16[192,1024]{1,0:T(8,128)(2,1)S(1)} %copy-done.14), channel_id=1, source_target_pairs={{0,1},{1,2},{2,3},{3,0},{4,5},{5,6},{6,7},{7,4},{8,9},{9,10},{10,1... | collective-permute-start | bytes 1179656 | tf_op jit(solution)/shard_map/ppermute | solution.py:471
  160.4 25.3 %copy-start.47 = (bf16[192,1024]{1,0:T(8,128)(2,1)}, bf16[192,1024]{1,0:T(8,128)(2,1)S(1)}, u32[]{:S(2)}) copy-start(bf16[192,1024]{1,0:T(8,128)(2,1)S(1)} %collective-permute-done.7) | copy-start | bytes 1179652
  199.4 29.0 %all-to-all-start.3 = ((bf16[8,1,160,768]{3,2,1,0:T(8,128)(2,1)}), bf16[8,1,160,768]{3,2,1,0:T(8,128)(2,1)}, u32[]{:S(2)}, u32[]{:S(2)}) async-start(bf16[8,1,160,768]{3,2,1,0:T(8,128)(2,1)} %bitcast.111), calls=%async_computation.3 | async-start | bytes 3932160 | tf_op jit(solution)/shard_map/all_to_all | solution.py:392
  209.3 23.7 %copy-start.28 = (bf16[2,96,512]{2,1,0:T(8,128)(2,1)S(1)}, bf16[2,96,512]{2,1,0:T(8,128)(2,1)}, u32[]{:S(2)}) copy-start(bf16[2,96,512]{2,1,0:T(8,128)(2,1)} %param.23) | copy-start | bytes 589828
  228.4 32.0 %all-to-all-start.4 = ((bf16[8,1,160,768]{3,2,1,0:T(8,128)(2,1)}), bf16[8,1,160,768]{3,2,1,0:T(8,128)(2,1)}, u32[]{:S(2)}, u32[]{:S(2)}) async-start(bf16[8,1,160,768]{3,2,1,0:T(8,128)(2,1)} %bitcast.109), calls=%async_computation.4 | async-start | bytes 3932160 | tf_op jit(solution)/shard_map/all_to_all | solution.py:392
  232.9 66.6 %all-gather.5.cloned.1.call-start = ((), (), s32[]{:S(2)}) async-start(), calls=%async_computation.14 | async-start | bytes 2654208 | tf_op jit(solution)/shard_map/all_gather | solution.py:491
  260.4 28.9 %all-to-all-start.5 = ((bf16[8,1,160,768]{3,2,1,0:T(8,128)(2,1)}), bf16[8,1,160,768]{3,2,1,0:T(8,128)(2,1)}, u32[]{:S(2)}, u32[]{:S(2)}) async-start(bf16[8,1,160,768]{3,2,1,0:T(8,128)(2,1)} %get-tuple-element.95), calls=%async_computation.5 | async-start | bytes 3932160 | tf_op jit(solution)/shard_map/all_to_all | solution.py:392
  289.3 29.1 %all-to-all-start.6 = ((bf16[8,1,160,768]{3,2,1,0:T(8,128)(2,1)}), bf16[8,1,160,768]{3,2,1,0:T(8,128)(2,1)}, u32[]{:S(2)}, u32[]{:S(2)}) async-start(bf16[8,1,160,768]{3,2,1,0:T(8,128)(2,1)} %get-tuple-element.96), calls=%async_computation.6 | async-start | bytes 3932160 | tf_op jit(solution)/shard_map/all_to_all | solution.py:392
  354.2 28.6 %all-to-all-start.8 = ((bf16[8,1,160,768]{3,2,1,0:T(8,128)(2,1)}), bf16[8,1,160,768]{3,2,1,0:T(8,128)(2,1)}, u32[]{:S(2)}, u32[]{:S(2)}) async-start(bf16[8,1,160,768]{3,2,1,0:T(8,128)(2,1)} %get-tuple-element.105), calls=%async_computation.8 | async-start | bytes 3932160 | tf_op jit(solution)/shard_map/all_to_all | solution.py:392
  358.6 71.9 %all-reduce.6.cloned.1.call-start = ((), (), s32[]{:S(2)}) async-start(), calls=%async_computation.15 | async-start | bytes 3145728 | tf_op jit(solution)/shard_map/psum | solution.py:549
  463.3 63.9 %all-to-all-start.9 = ((bf16[8,3,96,512]{3,2,1,0:T(8,128)(2,1)}), bf16[8,3,96,512]{3,2,1,0:T(8,128)(2,1)}, u32[]{:S(2)}, u32[]{:S(2)}) async-start(bf16[8,3,96,512]{3,2,1,0:T(8,128)(2,1)} %pad_maximum_fusion.2), calls=%async_computation.9 | async-start | bytes 4718592 | tf_op jit(solution)/shard_map/all_to_all | solution.py:557
  483.5 39.2 %collective-permute-start.9 = (bf16[384,1024]{1,0:T(8,128)(2,1)S(1)}, bf16[384,1024]{1,0:T(8,128)(2,1)S(1)}, u32[]{:S(2)}, u32[]{:S(2)}) collective-permute-start(bf16[384,1024]{1,0:T(8,128)(2,1)S(1)} %get-tuple-element.206), channel_id=1, source_target_pairs={{8,0},{12,4},{9,1},{13,5},{10,2},{14,6},{11,3},{15,7},{24,16},{28,... | collective-permute-start | bytes 2359304 | tf_op jit(solution)/shard_map/ppermute | solution.py:579
  485.0 37.8 %collective-permute-start.8 = (bf16[384,1024]{1,0:T(8,128)(2,1)S(1)}, bf16[384,1024]{1,0:T(8,128)(2,1)S(1)}, u32[]{:S(2)}, u32[]{:S(2)}) collective-permute-start(bf16[384,1024]{1,0:T(8,128)(2,1)S(1)} %get-tuple-element.205), channel_id=1, source_target_pairs={{4,0},{8,4},{12,8},{5,1},{9,5},{13,9},{6,2},{10,6},{14,10},{7,3},{... | collective-permute-start | bytes 2359304 | tf_op jit(solution)/shard_map/ppermute | solution.py:579
  527.2 29.8 %all-to-all-start.10 = ((bf16[4,2,192,512]{3,2,1,0:T(8,128)(2,1)}), bf16[4,2,192,512]{3,2,1,0:T(8,128)(2,1)}, u32[]{:S(2)}, u32[]{:S(2)}) async-start(bf16[4,2,192,512]{3,2,1,0:T(8,128)(2,1)} %pad_maximum_fusion.3), calls=%async_computation.10 | async-start | bytes 3145728 | tf_op jit(solution)/shard_map/all_to_all | solution.py:520
  536.8 73.4 %all-reduce.8.cloned.1.call-start = ((), (), s32[]{:S(2)}) async-start(), calls=%async_computation.16 | async-start | bytes 3145728 | tf_op jit(solution)/shard_map/psum | solution.py:569
  557.0 57.1 %all-to-all-start.11 = ((bf16[8,96,786]{2,1,0:T(8,128)(2,1)}), bf16[8,96,786]{2,1,0:T(8,128)(2,1)}, u32[]{:S(2)}, u32[]{:S(2)}) async-start(bf16[8,96,786]{2,1,0:T(8,128)(2,1)} %bitcast.99), calls=%async_computation.11 | async-start | bytes 2752512 | tf_op jit(solution)/shard_map/all_to_all | solution.py:325
  561.2 120.8 %all-reduce.10.cloned.1.call-start = ((), (), s32[]{:S(2)}) async-start(), calls=%async_computation.17 | async-start | bytes 3145728 | tf_op jit(solution)/shard_map/psum | solution.py:589
  615.6 76.5 %all-to-all-start.12 = ((bf16[4,2,2,192,512]{4,3,2,1,0:T(8,128)(2,1)}), bf16[4,2,2,192,512]{4,3,2,1,0:T(8,128)(2,1)}, u32[]{:S(2)}, u32[]{:S(2)}) async-start(bf16[4,2,2,192,512]{4,3,2,1,0:T(8,128)(2,1)} %pad_maximum_fusion.1), calls=%async_computation.12 | async-start | bytes 6291456 | tf_op jit(solution)/shard_map/all_to_all | solution.py:520
  629.8 58.4 %copy-start = (f32[1024,768]{1,0:T(8,128)S(1)}, f32[1024,768]{1,0:T(8,128)}, u32[]{:S(2)}) copy-start(f32[1024,768]{1,0:T(8,128)} %multiply_add_fusion) | copy-start | bytes 9437188
  (47 other events, 239.4 us)
Sparse Core Ops, SparseCore 0:
  89.4 46.0 all-gather.2
  236.2 32.0 all-gather.4
  362.3 68.0 all-reduce.5
  540.2 69.9 all-reduce.7
  612.4 69.5 all-reduce.9
